TPU v7x, 32 devices: a whole 2x2x4 slice. The times are simulated.
32 devices in a mesh: dp: 4 (over y, x), ctx: 4 (over z), tensor: 2 (over core).
Axes of the slice: x: 2, y: 2, z: 4, core: 2. Of those that a mesh axis runs over, the one named last changes fastest.
Arguments:
- tokens: bfloat16 [8, 2048, 1536], P('dp', 'ctx'), may hold values from -6 to 6
- cotangent: bfloat16 [8, 2048, 1536], P('dp', 'ctx'), may hold values from -6 to 6
- lengths: int32 [8], P('dp'), may hold values from 512 to 2048, as said below
- slot_adapter_index: int32 [8], P('dp'), may hold values from 0 to 7
- input_norm_gain: float32 [1536], replicated, may hold values from 0.5 to 1.5
- gate_weight_matrix: bfloat16 [1536, 3072], P('dp', 'tensor'), may hold values from -0.15625 to 0.15625
- inner_weight_matrix: bfloat16 [1536, 3072], P('dp', 'tensor'), may hold values from -0.15625 to 0.15625
- state_map_weight: bfloat16 [1536, 256], P('dp'), may hold values from -0.15625 to 0.15625
- step_size_weight: bfloat16 [1536, 48], P('dp', 'tensor'), may hold values from -0.15625 to 0.15625
- output_projection_weight: bfloat16 [1536, 3072], P('dp', 'tensor'), may hold values from -0.109375 to 0.109375
- inner_channel_taps: float32 [4, 3072], P(None, 'tensor'), may hold values from -3 to 3
- state_map_taps: float32 [4, 256], replicated, may hold values from -3 to 3
- inner_conv_bias: float32 [3072], P('tensor'), may hold values from -2 to 2
- state_map_conv_bias: float32 [256], replicated, may hold values from -2 to 2
- step_size_bias: float32 [48], P('tensor'), may hold values from -2 to 0
- log_decay_rate: float32 [48], P('tensor'), may hold values from -12 to -2
- head_skip_gain: float32 [48], P('tensor'), may hold values from 0.5 to 1.5
- gated_norm_gain: float32 [3072], P('tensor'), may hold values from 0.5 to 1.5
- adapter_in_down_maps: bfloat16 [8, 1536, 16], replicated, may hold values from -0.15625 to 0.15625
- adapter_in_up_maps: bfloat16 [8, 2, 16, 3072], P(None, None, None, 'tensor'), may hold values from -1.5 to 1.5
- adapter_out_down_maps: bfloat16 [8, 3072, 16], P(None, 'tensor'), may hold values from -0.109375 to 0.109375
- adapter_out_up_maps: bfloat16 [8, 16, 1536], replicated, may hold values from -1.5 to 1.5
Outputs:
- result: bfloat16 [8, 2048, 1536], P('dp', 'ctx')
- grad_tokens: float32 [8, 2048, 1536], P('dp', 'ctx')
- grad_lora_in_down: float32 [8, 1536, 16], replicated
- grad_lora_in_up: float32 [8, 2, 16, 3072], P(None, None, None, 'tensor')
- grad_lora_out_down: float32 [8, 3072, 16], P(None, 'tensor')
- grad_lora_out_up: float32 [8, 16, 1536], replicated
Inputs may be any that keep to these rules, and one draw needn't show every extreme that they name: Each slot holds one sequence in its first lengths positions; in every draw some slot has length 2048.
All inputs are finite; a program needn't handle non-finite values.
Results may differ from a plain program's by a relative error of at most 0.006.
The roundings to bfloat16 on the way count: a program that leaves them out, or rounds other values in their place, can miss the bound.
Values may be sent and summed in bfloat16 or wider, within the bound.
A program may use at most 320 MiB of HBM per device.

v0:
```python
import jax
import jax.numpy as jnp
from jax import lax
from jax.sharding import PartitionSpec as P

MIXER_WIDTH = 3072
GROUP = 256


EPSILON = 1e-05
HIGH_PRECISION = lax.Precision.HIGH


def shifted(block, axis, distance):
    devices = range(lax.axis_size(axis))
    route = [(i - distance, i) for i in devices if i - distance in devices]
    return lax.ppermute(block, axis, route)


def carried_in(value, axis, join, neutral):
    count, mine = (lax.axis_size(axis), lax.axis_index(axis))
    pieces = jax.tree.map(lambda part: lax.all_gather(part, axis), value)
    total = jax.tree.map(
        lambda part, zero: jnp.full_like(part, 0) + jnp.asarray(zero, part.dtype), value, neutral
    )

    def lap(position, total):
        longer = join(total, jax.tree.map(lambda part: part[position], pieces))
        return jax.tree.map(lambda new, old: jnp.where(position < mine, new, old), longer, total)

    return lax.fori_loop(0, count - 1, lap, total)


def entering(array, axis, join, neutral):
    count = lax.axis_size(axis)
    place = lax.axis_index(axis)
    ahead = count - 1 - place
    gathered = jax.tree.map(
        lambda a, kind: lax.all_gather(a.astype(kind), axis), array, (jnp.bfloat16, jnp.bfloat16)
    )
    state = jax.tree.map(lambda a, e: jnp.zeros_like(a) + jnp.asarray(e, a.dtype), array, neutral)

    def one(lap, state):
        source = count - 1 - lap
        return join(
            state,
            jax.tree.map(
                lambda a, own: lax.dynamic_index_in_dim(a, source, 0, False).astype(own.dtype),
                gathered,
                array,
            ),
        )

    return lax.fori_loop(0, ahead, one, state)


def for_sending(array):
    return jax.tree.map(lambda a: a.astype(jnp.bfloat16) if a.dtype == jnp.float32 else a, array)


def silu_grad(value):
    sigmoid_val = jax.nn.sigmoid(value)
    return sigmoid_val * (1.0 + value * (1.0 - sigmoid_val))


def chain_link(earlier, latter):
    return (earlier[0] * latter[0], latter[0][..., None, None] * earlier[1] + latter[1])


def on_device(
    tokens,
    cotangent,
    lengths,
    slot_adapter_index,
    input_norm_gain,
    gate_weight_matrix,
    inner_weight_matrix,
    state_map_weight,
    step_size_weight,
    output_projection_weight,
    inner_channel_taps,
    state_map_taps,
    inner_conv_bias,
    state_map_conv_bias,
    step_size_bias,
    log_decay_rate,
    head_skip_gain,
    gated_norm_gain,
    adapter_in_down_maps,
    adapter_in_up_maps,
    adapter_out_down_maps,
    adapter_out_up_maps,
):
    slot_count, length, model_width = tokens.shape
    inner_width = gate_weight_matrix.shape[1]
    head_count = step_size_bias.shape[0]
    head_dim = inner_width // head_count
    states = state_map_weight.shape[1] // 2
    tap_count = inner_channel_taps.shape[0]
    blocks = length // GROUP
    adapter_set = adapter_in_down_maps.shape[0]
    weights = (
        gate_weight_matrix,
        inner_weight_matrix,
        state_map_weight,
        step_size_weight,
        output_projection_weight,
    )
    gate_full, inner_full, bc_full, step_full, out_full = (
        lax.all_gather(weights[0], "dp", axis=0, tiled=True),
        lax.all_gather(weights[1], "dp", axis=0, tiled=True),
        lax.all_gather(weights[2], "dp", axis=0, tiled=True),
        lax.all_gather(weights[3], "dp", axis=0, tiled=True),
        lax.all_gather(weights[4], "dp", axis=0, tiled=True),
    )
    places = lax.axis_index("ctx") * length + jnp.arange(length, dtype=jnp.int32)
    live_mask = (places[None, :] < lengths[:, None]).astype(jnp.float32)
    adapter_selector = (
        slot_adapter_index[:, None] == jnp.arange(adapter_set, dtype=jnp.int32)[None, :]
    ).astype(jnp.bfloat16)
    in_down = jnp.einsum(
        "tp,pvm->tvm", adapter_selector, adapter_in_down_maps, preferred_element_type=jnp.float32
    ).astype(jnp.bfloat16)
    in_up = jnp.einsum(
        "wg,ghnl->whnl", adapter_selector, adapter_in_up_maps, preferred_element_type=jnp.float32
    ).astype(jnp.bfloat16)
    out_down = jnp.einsum(
        "ow,wel->oel", adapter_selector, adapter_out_down_maps, preferred_element_type=jnp.float32
    ).astype(jnp.bfloat16)
    out_up = jnp.einsum(
        "xw,whm->xhm", adapter_selector, adapter_out_up_maps, preferred_element_type=jnp.float32
    ).astype(jnp.bfloat16)
    tok_float = tokens.astype(jnp.float32)
    in_scale = lax.rsqrt(jnp.mean(tok_float * tok_float, axis=-1, keepdims=True) + EPSILON)
    normed = (tok_float * in_scale * input_norm_gain).astype(jnp.bfloat16)
    low_in = jnp.einsum("std,sdr->str", normed, in_down, preferred_element_type=jnp.float32).astype(
        jnp.bfloat16
    )
    gate_val = jnp.einsum(
        "std,dc->stc", normed, gate_full, preferred_element_type=jnp.float32
    ) + jnp.einsum("str,src->stc", low_in, in_up[:, 0], preferred_element_type=jnp.float32)
    inner_val = jnp.einsum(
        "std,dc->stc", normed, inner_full, preferred_element_type=jnp.float32
    ) + jnp.einsum("str,src->stc", low_in, in_up[:, 1], preferred_element_type=jnp.float32)
    bc_val = jnp.einsum("std,dc->stc", normed, bc_full, preferred_element_type=jnp.float32)
    step_raw = jnp.einsum("std,dc->stc", normed, step_full, preferred_element_type=jnp.float32)
    conv_input = jnp.concatenate([inner_val, bc_val], axis=-1).astype(jnp.bfloat16)
    edge_rows = shifted(conv_input[:, length - (tap_count - 1) :], "ctx", 1)
    extended = jnp.concatenate([edge_rows, conv_input], axis=1).astype(jnp.float32)
    conv_weight = jnp.concatenate([inner_channel_taps, state_map_taps], axis=1)
    conv_bias = jnp.concatenate([inner_conv_bias, state_map_conv_bias])
    conv_val = jnp.zeros(conv_input.shape, jnp.float32) + conv_bias
    for offset in range(tap_count):
        conv_val = conv_val + conv_weight[offset] * extended[:, offset : offset + length]
    activated = jax.nn.silu(conv_val)
    x_block = (
        activated[..., :inner_width]
        .astype(jnp.bfloat16)
        .reshape(slot_count, blocks, GROUP, head_count, head_dim)
    )
    b_block = (
        activated[..., inner_width : inner_width + states]
        .astype(jnp.bfloat16)
        .reshape(slot_count, blocks, GROUP, states)
    )
    c_block = (
        activated[..., inner_width + states :]
        .astype(jnp.bfloat16)
        .reshape(slot_count, blocks, GROUP, states)
    )
    step_val = jax.nn.softplus(step_raw + step_size_bias)
    decay_rate = -jnp.exp(log_decay_rate)
    step_block = step_val.reshape(slot_count, blocks, GROUP, head_count).transpose(0, 1, 3, 2)
    cumulative = jnp.cumsum(step_block * decay_rate[None, None, :, None], axis=-1)
    position = jnp.arange(GROUP)
    causal = position[:, None] >= position[None, :]
    spread_log = jnp.where(causal, cumulative[..., :, None] - cumulative[..., None, :], 0.0)
    decay_table = jnp.where(causal, jnp.exp(spread_log), 0.0)
    scores = jnp.einsum("scqn,sckn->scqk", c_block, b_block, preferred_element_type=jnp.float32)
    mixing = (scores[:, :, None] * decay_table * step_block[..., None, :]).astype(jnp.bfloat16)
    inside = jnp.einsum("schqk,sckhp->scqhp", mixing, x_block, preferred_element_type=jnp.float32)
    tail_weight = jnp.exp(cumulative[..., -1:] - cumulative) * step_block
    weighted_x = x_block.astype(jnp.float32) * tail_weight.transpose(0, 1, 3, 2)[..., None]
    fresh_state = jnp.einsum(
        "sckhp,sckn->schpn", weighted_x, b_block.astype(jnp.float32), precision=HIGH_PRECISION
    )
    block_decay = jnp.exp(cumulative[..., -1])
    local_state = jnp.zeros((slot_count, head_count, head_dim, states), jnp.float32)
    for number in range(blocks):
        local_state = block_decay[:, number, :, None, None] * local_state + fresh_state[:, number]
    device_decay = jnp.prod(block_decay, axis=1)
    incoming = carried_in(
        (device_decay, local_state),
        "ctx",
        chain_link,
        (jnp.ones_like(device_decay), jnp.zeros_like(local_state)),
    )[1]
    starts = []
    running = incoming
    for number in range(blocks):
        starts.append(running)
        running = block_decay[:, number, :, None, None] * running + fresh_state[:, number]
    start_states = jnp.stack(starts, axis=1)
    rise_factor = jnp.exp(cumulative).transpose(0, 1, 3, 2)
    carried_raw = jnp.einsum(
        "scqn,schpn->scqhp", c_block.astype(jnp.float32), start_states, precision=HIGH_PRECISION
    )
    carried = carried_raw * rise_factor[..., None]
    mixer_out = (inside + carried + head_skip_gain[:, None] * x_block.astype(jnp.float32)).reshape(
        slot_count, length, inner_width
    )
    silu_gate = jax.nn.silu(gate_val)
    gated_val = mixer_out * silu_gate
    square_sum = lax.psum(jnp.sum(gated_val * gated_val, axis=-1), "tensor")
    gate_scale = lax.rsqrt(square_sum / MIXER_WIDTH + EPSILON)[..., None]
    normed_out = (gated_val * gate_scale * gated_norm_gain).astype(jnp.bfloat16)
    partial_out = jnp.einsum(
        "stc,dc->std", normed_out, out_full, preferred_element_type=jnp.float32
    )
    partial_low = jnp.einsum(
        "stc,scr->str", normed_out, out_down, preferred_element_type=jnp.float32
    )
    branch_total, low_total = lax.psum((partial_out, partial_low), "tensor")
    low_out = low_total.astype(jnp.bfloat16)
    branch = branch_total + jnp.einsum(
        "str,srd->std", low_out, out_up, preferred_element_type=jnp.float32
    )
    result = (tok_float + live_mask[..., None] * branch).astype(jnp.bfloat16)
    gate_full, inner_full, bc_full, step_full, out_full = (
        lax.all_gather(weights[0], "dp", axis=0, tiled=True),
        lax.all_gather(weights[1], "dp", axis=0, tiled=True),
        lax.all_gather(weights[2], "dp", axis=0, tiled=True),
        lax.all_gather(weights[3], "dp", axis=0, tiled=True),
        lax.all_gather(weights[4], "dp", axis=0, tiled=True),
    )
    grad_branch = (cotangent.astype(jnp.float32) * live_mask[..., None]).astype(jnp.bfloat16)
    grad_low_out = jnp.einsum(
        "std,srd->str", grad_branch, out_up, preferred_element_type=jnp.float32
    )
    up_out_grad = jnp.einsum(
        "str,std->srd", low_out, grad_branch, preferred_element_type=jnp.float32
    )
    grad_normed = jnp.einsum(
        "std,dc->stc", grad_branch, out_full, preferred_element_type=jnp.float32
    ) + jnp.einsum(
        "str,scr->stc", grad_low_out, out_down.astype(jnp.float32), precision=HIGH_PRECISION
    )
    down_out_grad = jnp.einsum(
        "stc,str->scr", normed_out.astype(jnp.float32), grad_low_out, precision=HIGH_PRECISION
    )
    weighted = grad_normed * gated_norm_gain
    cross_sum = lax.psum(jnp.sum(gated_val * weighted, axis=-1), "tensor")
    grad_gated = (
        gate_scale * weighted - gated_val * gate_scale**3 * (cross_sum / MIXER_WIDTH)[..., None]
    )
    grad_mixer = (grad_gated * silu_gate).astype(jnp.bfloat16)
    grad_gate = (grad_gated * mixer_out * silu_grad(gate_val)).astype(jnp.bfloat16)
    grad_y = grad_mixer.reshape(slot_count, blocks, GROUP, head_count, head_dim)
    grad_y_float = grad_y.astype(jnp.float32)
    b_float = b_block.astype(jnp.float32)
    c_float = c_block.astype(jnp.float32)
    grad_mix = jnp.einsum("scqhp,sckhp->schqk", grad_y, x_block, preferred_element_type=jnp.float32)
    grad_x = (
        jnp.einsum("schqk,scqhp->sckhp", mixing, grad_y, preferred_element_type=jnp.float32)
        + head_skip_gain[:, None] * grad_y_float
    )
    through = grad_mix * decay_table * scores[:, :, None]
    grad_scores = jnp.sum(grad_mix * decay_table * step_block[..., None, :], axis=2)
    grad_c = jnp.einsum("scqk,sckn->scqn", grad_scores, b_float, precision=HIGH_PRECISION)
    grad_b = jnp.einsum("scqk,scqn->sckn", grad_scores, c_float, precision=HIGH_PRECISION)
    grad_step = jnp.sum(through, axis=-2)
    along = through * step_block[..., None, :]
    grad_cumul = jnp.sum(along, axis=-1) - jnp.sum(along, axis=-2)
    scaled_grad = grad_y_float * rise_factor[..., None]
    grad_c = grad_c + jnp.einsum(
        "scqhp,schpn->scqn", scaled_grad, start_states, precision=HIGH_PRECISION
    )
    local_grad = jnp.einsum("scqhp,scqn->schpn", scaled_grad, c_float, precision=HIGH_PRECISION)
    grad_cumul = grad_cumul + jnp.sum(grad_y_float * carried, axis=-1).transpose(0, 1, 3, 2)
    pending = jnp.zeros_like(local_state)
    for number in reversed(range(blocks)):
        pending = local_grad[:, number] + block_decay[:, number, :, None, None] * pending
    later_grad = entering(
        (device_decay, pending),
        "ctx",
        chain_link,
        (jnp.ones_like(device_decay), jnp.zeros_like(pending)),
    )[1]
    following = []
    running = later_grad
    for number in reversed(range(blocks)):
        following.append(running)
        running = local_grad[:, number] + block_decay[:, number, :, None, None] * running
    grad_fresh = jnp.stack(following[::-1], axis=1)
    grad_block_decay = jnp.sum(grad_fresh * start_states, axis=(-2, -1))
    state_by_b = jnp.einsum("schpn,sckn->sckhp", grad_fresh, b_float, precision=HIGH_PRECISION)
    grad_x = grad_x + state_by_b * tail_weight.transpose(0, 1, 3, 2)[..., None]
    grad_b = grad_b + jnp.einsum(
        "sckhp,schpn->sckn", weighted_x, grad_fresh, precision=HIGH_PRECISION
    )
    grad_tail = jnp.sum(state_by_b * x_block.astype(jnp.float32), axis=-1).transpose(0, 1, 3, 2)
    grad_step = grad_step + grad_tail * jnp.exp(cumulative[..., -1:] - cumulative)
    tail_pull = grad_tail * tail_weight
    end_pull = jnp.sum(tail_pull, axis=-1) + grad_block_decay * block_decay
    grad_cumul = (grad_cumul - tail_pull).at[..., -1].add(end_pull)
    grad_log_step = jnp.flip(jnp.cumsum(jnp.flip(grad_cumul, -1), axis=-1), -1)
    grad_step = grad_step + grad_log_step * decay_rate[None, None, :, None]
    grad_step_raw = (
        grad_step.transpose(0, 1, 3, 2).reshape(slot_count, length, head_count)
        * jax.nn.sigmoid(step_raw + step_size_bias)
    ).astype(jnp.bfloat16)
    grad_act = jnp.concatenate(
        [
            grad_x.reshape(slot_count, length, inner_width),
            grad_b.reshape(slot_count, length, states),
            grad_c.reshape(slot_count, length, states),
        ],
        axis=-1,
    )
    grad_conv = grad_act * silu_grad(conv_val)
    grad_ext = jnp.zeros((slot_count, length + tap_count - 1, grad_conv.shape[-1]), jnp.float32)
    for offset in range(tap_count):
        grad_ext = grad_ext + jnp.pad(
            conv_weight[offset] * grad_conv, ((0, 0), (offset, tap_count - 1 - offset), (0, 0))
        )
    back_edges = shifted(for_sending(grad_ext[:, : tap_count - 1]), "ctx", -1)
    grad_pre = grad_ext[:, tap_count - 1 :] + jnp.pad(
        back_edges, ((0, 0), (length - (tap_count - 1), 0), (0, 0))
    )
    grad_inner = grad_pre[..., :inner_width].astype(jnp.bfloat16)
    grad_bc = grad_pre[..., inner_width:]
    grad_low_in = jnp.einsum(
        "stc,src->str", grad_gate, in_up[:, 0], preferred_element_type=jnp.float32
    ) + jnp.einsum("stc,src->str", grad_inner, in_up[:, 1], preferred_element_type=jnp.float32)
    up_in_grad = jnp.stack(
        [
            jnp.einsum("str,stc->src", low_in, grad_gate, preferred_element_type=jnp.float32),
            jnp.einsum("str,stc->src", low_in, grad_inner, preferred_element_type=jnp.float32),
        ],
        axis=1,
    )
    partial_in = (
        jnp.einsum("stc,dc->std", grad_gate, gate_full, preferred_element_type=jnp.float32)
        + jnp.einsum("stc,dc->std", grad_inner, inner_full, preferred_element_type=jnp.float32)
        + jnp.einsum("stc,dc->std", grad_step_raw, step_full, preferred_element_type=jnp.float32)
        + jnp.einsum("stc,dc->std", grad_bc, bc_full.astype(jnp.float32), precision=HIGH_PRECISION)
    )
    grad_normed_in, grad_low_sum = lax.psum((partial_in, grad_low_in), "tensor")
    grad_normed_in = grad_normed_in + jnp.einsum(
        "str,sdr->std", grad_low_sum, in_down.astype(jnp.float32), precision=HIGH_PRECISION
    )
    down_in_grad = jnp.einsum(
        "std,str->sdr", normed.astype(jnp.float32), grad_low_sum, precision=HIGH_PRECISION
    )
    weighted_in = grad_normed_in * input_norm_gain
    grad_tokens = (
        cotangent.astype(jnp.float32)
        + in_scale * weighted_in
        - tok_float * in_scale**3 * jnp.mean(tok_float * weighted_in, axis=-1, keepdims=True)
    )
    picker_float = adapter_selector.astype(jnp.float32)
    table_grads = (
        jnp.einsum("sa,sdr->adr", picker_float, down_in_grad),
        jnp.einsum("sa,sqrc->aqrc", picker_float, up_in_grad),
        jnp.einsum("sa,scr->acr", picker_float, down_out_grad),
        jnp.einsum("sa,srd->ard", picker_float, up_out_grad),
    )
    summed = lax.psum(
        (table_grads[0], table_grads[1], table_grads[2], table_grads[3]), ("dp", "ctx")
    )
    return (result, grad_tokens, summed[0], summed[1], summed[2], summed[3])


def solution(mesh):
    in_specs = (
        P("dp", "ctx", None),
        P("dp", "ctx", None),
        P("dp"),
        P("dp"),
        P(),
        P("dp", "tensor"),
        P("dp", "tensor"),
        P("dp", None),
        P("dp", "tensor"),
        P("dp", "tensor"),
        P(None, "tensor"),
        P(),
        P("tensor"),
        P(),
        P("tensor"),
        P("tensor"),
        P("tensor"),
        P("tensor"),
        P(),
        P(None, None, None, "tensor"),
        P(None, "tensor", None),
        P(),
    )
    out_specs = (
        P("dp", "ctx", None),
        P("dp", "ctx", None),
        P(),
        P(None, None, None, "tensor"),
        P(None, "tensor", None),
        P(),
    )
    return jax.shard_map(
        on_device, mesh=mesh, in_specs=in_specs, out_specs=out_specs, check_vma=False
    )
```

profile of v0, /device:TPU:0, one launch (start us, length us, event | category | flops | bytes accessed | tf_op | source)
XLA Modules:
  0.0 837.0 jit_solution(7290837645645209631)
XLA Ops:
  12.8 10.0 %all_gather.40 = bf16[1536,24]{0,1:T(8,128)(2,1)S(1)} all-gather(bf16[384,24]{0,1:T(8,128)(2,1)S(1)} %copy-done.87), channel_id=1, replica_groups=mesh['dp'=4,'ctx'=4,'tensor'=2] {'dp'}, dimensions={0}, use_global_device_ids=true | all-gather | bytes 92160 | tf_op jit(solution)/shard_map/all_gather | solution.py:113
  34.5 18.9 %all_gather.39 = bf16[1536,256]{0,1:T(8,128)(2,1)S(1)} all-gather(bf16[384,256]{0,1:T(8,128)(2,1)S(1)} %copy.353), channel_id=1, replica_groups=mesh['dp'=4,'ctx'=4,'tensor'=2] {'dp'}, dimensions={0}, use_global_device_ids=true | all-gather | bytes 983040 | tf_op jit(solution)/shard_map/all_gather | solution.py:112
  62.8 9.6 %all-gather.10.cloned.1.call-done = bf16[1536,1536]{1,0:T(8,128)(2,1)} async-done(((bf16[384,1536]{1,0:T(8,128)(2,1)}), bf16[1536,1536]{1,0:T(8,128)(2,1)}) %all-gather.10.cloned.1.call-update) | async-done | bytes 4718608 | tf_op jit(solution)/shard_map/all_gather | solution.py:111
  118.4 11.3 %all-gather.3 = bf16[4,2,24]{2,1,0:T(2,128)(2,1)} all-gather(bf16[1,2,24]{2,1,0:T(2,128)(2,1)S(1)} %convert_bitcast_fusion), channel_id=3, replica_groups=mesh['dp'=4,'ctx'=4,'tensor'=2] {'ctx'}, dimensions={0}, use_global_device_ids=true | all-gather | bytes 480 | tf_op jit(solution)/shard_map/all_gather | solution.py:39
  160.1 29.9 %all-gather.16.cloned.1.call-done = bf16[1536,1536]{1,0:T(8,128)(2,1)} async-done(((bf16[384,1536]{1,0:T(8,128)(2,1)}), bf16[1536,1536]{1,0:T(8,128)(2,1)}) %all-gather.16.cloned.1.call-update) | async-done | bytes 4718608 | tf_op jit(solution)/shard_map/all_gather | solution.py:114
  190.0 9.7 %fusion.26 = f32[2,512,1536]{2,1,0:T(8,128)} fusion(bf16[1536,1536]{1,0:T(8,128)(2,1)} %all-gather.16.cloned.1.call-done, bf16[2,512,1536]{2,1,0:T(8,128)(2,1)} %param.29, f32[2,512]{1,0:T(2,128)S(1)} %compare_convert_fusion), kind=kOutput, calls=%fused_computation.71 | convolution fusion | flops 4836556800 | bytes 14159872 | tf_op jit(solution)/shard_map/std,dc->stc/dot_general | solution.py:243
  201.0 106.3 %all-gather.12.cloned.1.call-done = f32[4,2,24,64,128]{4,3,2,1,0:T(8,128)} async-done(((f32[1,2,24,64,128]{4,3,2,1,0:T(8,128)}), f32[4,2,24,64,128]{4,3,2,1,0:T(8,128)}) %all-gather.12.cloned.1.call-update) | async-done | bytes 6291472 | tf_op jit(solution)/shard_map/all_gather | solution.py:22
  319.2 10.2 %fusion.12 = f32[2,2,256,24,64]{2,4,3,1,0:T(8,128)} fusion(bf16[2,2,256,24,64]{2,4,3,1,0:T(8,128)(2,1)S(1)} %copy-done.13, f32[2,2,256,24,64]{2,4,3,1,0:T(8,128)S(1)} %fusion.45, f32[24]{0:T(128)S(1)} %copy-done.105, f32[2,2,256,24]{2,3,1,0:T(8,128)S(1)} %copy-done.49, f32[2,2,24,256]{3,2,1,0:T(8,128)S(1)} %copy-done.63, ...), kind=kOutput, calls=%fused_computation.44 | convolution fusion | flops 850919424 | bytes 17137760 | tf_op jit(solution)/shard_map/schqk,sckhp->scqhp/dot_general | solution.py:181
  329.4 9.7 %copy.436 = f32[2,2,256,24,64]{4,3,2,1,0:T(8,128)} copy(f32[2,2,256,24,64]{2,4,3,1,0:T(8,128)} %fusion.12) | data formatting | bytes 12582912 | tf_op jit(solution)/shard_map/reshape | solution.py:209
  339.1 11.3 %reshape.304 = f32[2,512,1536]{2,1,0:T(8,128)} reshape(f32[2,2,256,24,64]{4,3,2,1,0:T(8,128)} %copy.436) | data formatting | bytes 12582912 | tf_op jit(solution)/shard_map/reshape | solution.py:209
  350.4 15.3 %multiply_reduce_fusion.4 = (f32[2,512]{1,0:T(2,128)S(1)}, f32[2,512]{1,0:T(2,128)S(1)}, f32[2,512,1536]{2,1,0:T(8,128)}, f32[2,512,1536]{2,1,0:T(8,128)}) fusion(f32[2,512,1536]{2,1,0:T(8,128)} %reshape.304, f32[2,512,1536]{2,1,0:T(8,128)} %convolution_add_fusion, f32[1536]{0:T(1024)S(1)} %copy-done.95, f32[2,512,1536]{2,1,0:T(8,128)} %fusion.26, ...), kind=kOutput, calls=%fused_computation.64 | convolution fusion | flops 168294400 | bytes 31635456 | tf_op jit(solution)/shard_map/str,scr->stc/dot_general | solution.py:245
  379.6 13.1 %multiply_convert_fusion.5 = (bf16[2,512,1536]{2,1,0:T(8,128)(2,1)}, bf16[2,512,1536]{2,1,0:T(8,128)(2,1)}) fusion(f32[2,512,1536]{2,1,0:T(8,128)} %convolution_add_fusion, f32[2,512,1536]{2,1,0:T(8,128)} %reshape.304, f32[2,512]{1,0:T(2,128)S(1)} %broadcast_multiply_fusion.4, f32[2,512,1536]{2,1,0:T(8,128)} %get-tuple-element.299, ...), kind=kLoop, calls=%fused_computation.62 | loop fusion | flops 26738688 | bytes 31469568 | tf_op jit(solution)/shard_map/convert_element_type | solution.py:257
  419.9 18.6 %multiply_reduce_fusion.1 = (f32[2,2,24,256]{3,2,1,0:T(8,128)}, f32[2,2,24,256]{3,2,1,0:T(8,128)}, f32[2,2,24,256]{3,2,1,0:T(8,128)}, f32[2,2,256,256]{3,2,1,0:T(8,128)}) fusion(f32[2,2,24,256]{3,2,1,0:T(8,128)} %copy.359, f32[2,2,256,256]{3,2,1,0:T(8,128)} %fusion.135, f32[2,2,24,256]{3,2,1,0:T(8,128)} %copy-done.54, ...), kind=kOutput, calls=%fused_computation.9 | convolution fusion | flops 874176512 | bytes 8945664 | tf_op jit(solution)/shard_map/scqhp,sckhp->schqk/dot_general | solution.py:262
  454.3 9.5 %fusion.30 = f32[2,512,1536]{2,1,0:T(8,128)} fusion(bf16[2,512,1536]{2,1,0:T(8,128)(2,1)S(1)} %copy-done.10, bf16[1536,1536]{1,0:T(8,128)(2,1)} %all-gather.14.cloned.1.call-done), kind=kOutput, calls=%fused_computation.75 | convolution fusion | flops 4831838208 | bytes 14155776 | tf_op jit(solution)/shard_map/stc,dc->std/dot_general | solution.py:343
  471.1 10.5 %all-gather.18.cloned.1.call-done = bf16[4,2,24,64,128]{4,3,2,1,0:T(8,128)(2,1)} async-done(((bf16[1,2,24,64,128]{4,3,2,1,0:T(8,128)(2,1)}), bf16[4,2,24,64,128]{4,3,2,1,0:T(8,128)(2,1)}) %all-gather.18.cloned.1.call-update) | async-done | bytes 3145744 | tf_op jit(solution)/shard_map/all_gather | solution.py:39
  499.9 11.0 %fusion.15 = f32[2,2,256,24,64]{2,4,3,1,0:T(8,128)} fusion(bf16[2,2,256,24,64]{2,4,3,1,0:T(8,128)(2,1)S(1)} %copy-done.21, f32[2,2,256,24,64]{2,4,3,1,0:T(8,128)S(1)} %get-tuple-element.330, f32[24]{0:T(128)S(1)} %copy-done.105, f32[2,2,256,24]{2,3,1,0:T(8,128)S(1)} %copy-done.57, f32[2,2,24,256]{3,2,1,0:T(8,128)S(1)} %copy-done.64, ...), kind=kOutput, calls=%fused_computation.47 | convolution fusion | flops 850919424 | bytes 17137760 | tf_op jit(solution)/shard_map/schqk,scqhp->sckhp/dot_general | solution.py:264
  510.8 9.7 %copy.428 = f32[2,2,256,24,64]{4,3,2,1,0:T(8,128)} copy(f32[2,2,256,24,64]{2,4,3,1,0:T(8,128)} %fusion.15) | data formatting | bytes 12582912 | tf_op jit(solution)/shard_map/reshape | solution.py:314
  520.5 11.3 %reshape.302 = f32[2,512,1536]{2,1,0:T(8,128)} reshape(f32[2,2,256,24,64]{4,3,2,1,0:T(8,128)} %copy.428) | data formatting | bytes 12582912 | tf_op jit(solution)/shard_map/reshape | solution.py:314
  532.7 9.6 %broadcast_multiply_fusion.3 = (f32[2,512,1792]{2,1,0:T(8,128)}, f32[2,512,1792]{2,1,0:T(8,128)}) fusion(f32[1792]{0:T(1024)S(1)} %copy-done.73, f32[2,512,1792]{2,1,0:T(8,128)} %get-tuple-element.301, f32[2,512,128]{2,1,0:T(8,128)S(1)} %bitcast.242, f32[2,512,128]{2,1,0:T(8,128)S(1)} %bitcast.243, f32[2,512,1536]{2,1,0:T(8,128)} %reshape.302), kind=kLoop, calls=%fused_computation.88 | loop fusion | flops 20185088 | bytes 29367296 | tf_op jit(solution)/shard_map/mul | solution.py:324
  542.2 11.0 %broadcast_multiply_fusion.2 = (f32[2,512,1792]{2,1,0:T(8,128)}, f32[2,512,1792]{2,1,0:T(8,128)}, f32[2,512,1792]{2,1,0:T(8,128)}) fusion(f32[2,512,1792]{2,1,0:T(8,128)} %get-tuple-element.298, f32[1792]{0:T(1024)S(1)} %copy-done.71, f32[1792]{0:T(1024)S(1)} %copy-done.69, f32[1792]{0:T(1024)S(1)} %copy-done.67), kind=kLoop, calls=%fused_computation.87 | loop fusion | flops 5505024 | bytes 29381632 | tf_op jit(solution)/shard_map/mul | solution.py:324
  553.2 10.7 %pad_add_fusion = f32[2,515,1792]{2,1,0:T(8,128)S(1)} fusion(f32[2,512,1792]{2,1,0:T(8,128)} %get-tuple-element.306, f32[2,512,1792]{2,1,0:T(8,128)} %get-tuple-element.305, f32[2,512,1792]{2,1,0:T(8,128)} %get-tuple-element.304, f32[2,512,1792]{2,1,0:T(8,128)} %get-tuple-element.297), kind=kLoop, calls=%fused_computation.29 | loop fusion | flops 5537280 | bytes 36743168 | tf_op jit(solution)/shard_map/add | solution.py:323
  584.7 9.3 %fusion.34 = f32[2,512,1536]{2,1,0:T(8,128)S(1)} fusion(bf16[1536,1536]{1,0:T(8,128)(2,1)} %all-gather.10.cloned.1.call-done, f32[2,512,1792]{2,1,0:T(8,128)S(1)} %slice_add_fusion), kind=kOutput, calls=%fused_computation.79 | convolution fusion | flops 4831838208 | bytes 14155776 | tf_op jit(solution)/shard_map/stc,dc->std/dot_general | solution.py:344
  613.1 35.8 %all-reduce.13.cloned.1.call-done = (f32[2,512,1536]{2,1,0:T(8,128)}, f32[2,512,1536]{2,1,0:T(8,128)}, f32[2,512,16]{1,2,0:T(8,128)}) async-done(((f32[2,512,1536]{2,1,0:T(8,128)}, f32[2,512,1536]{2,1,0:T(8,128)}, f32[2,512,16]{1,2,0:T(8,128)}), (f32[2,512,1536]{2,1,0:T(8,128)}, f32[2,512,1536]{2,1,0:T(8,128)}, f32[2,512,16]{1,2,0:T(8,128)})) %all-reduce.13.cloned.1.call-update) | async-done | bytes 12648464 | tf_op jit(solution)/shard_map/psum | solution.py:223
  667.5 152.4 %all-reduce.11.cloned.1.call-done = (f32[8,1536,16]{1,0,2:T(8,128)}, f32[8,2,16,1536]{3,0,2,1:T(8,128)}, f32[8,1536,16]{1,0,2:T(8,128)}, f32[8,16,1536]{2,0,1:T(8,128)}) async-done(((f32[8,1536,16]{1,0,2:T(8,128)}, f32[8,2,16,1536]{3,0,2,1:T(8,128)}, f32[8,1536,16]{1,0,2:T(8,128)}, f32[8,16,1536]{2,0,1:T(8,128)}), (f32[8,1536,16]{1,0,2:T(8,128)}, f32[8,2,16,1536]{3,0,2,1:T(8,128)}, ...) | async-done | bytes 3932176 | tf_op jit(solution)/shard_map/psum | solution.py:368
  (377 shorter events, 278.3 us)
Async XLA Ops:
  7.2 65.1 %all-gather.10.cloned.1.call-start = ((), (), s32[]{:S(2)}) async-start(), calls=%async_computation | async-start | bytes 5898240 | tf_op jit(solution)/shard_map/all_gather | solution.py:111
  8.0 140.0 %all-gather.14.cloned.1.call-start = ((), (), s32[]{:S(2)}) async-start(), calls=%async_computation.2 | async-start | bytes 5898240 | tf_op jit(solution)/shard_map/all_gather | solution.py:110
  8.7 181.3 %all-gather.16.cloned.1.call-start = ((), (), s32[]{:S(2)}) async-start(), calls=%async_computation.3 | async-start | bytes 5898240 | tf_op jit(solution)/shard_map/all_gather | solution.py:114
  9.5 297.9 %all-gather.12.cloned.1.call-start = ((), (), s32[]{:S(2)}) async-start(), calls=%async_computation.1 | async-start | bytes 7864320 | tf_op jit(solution)/shard_map/all_gather | solution.py:22
  12.1 41.3 %copy-start.84 = (f32[4,1536]{1,0:T(4,128)S(1)}, f32[4,1536]{1,0:T(4,128)}, u32[]{:S(2)}) copy-start(f32[4,1536]{1,0:T(4,128)} %param.38) | copy-start | bytes 73732
  12.7 59.6 %copy-start.89 = (f32[2,512]{1,0:T(2,128)}, f32[2,512]{1,0:T(2,128)S(1)}, u32[]{:S(2)}) copy-start(f32[2,512]{1,0:T(2,128)S(1)} %get-tuple-element.321) | copy-start | bytes 12292
  12.8 40.7 %copy-start.98 = (f32[4,256]{1,0:T(4,128)S(1)}, f32[4,256]{1,0:T(4,128)}, u32[]{:S(2)}) copy-start(f32[4,256]{1,0:T(4,128)} %param.39) | copy-start | bytes 12292
  53.5 34.4 %copy-start.66 = (f32[1792]{0:T(1024)}, f32[1792]{0:T(1024)S(1)}, u32[]{:S(2)}) copy-start(f32[1792]{0:T(1024)S(1)} %get-tuple-element.265) | copy-start | bytes 21508
  53.6 34.4 %copy-start.68 = (f32[1792]{0:T(1024)}, f32[1792]{0:T(1024)S(1)}, u32[]{:S(2)}) copy-start(f32[1792]{0:T(1024)S(1)} %get-tuple-element.266) | copy-start | bytes 21508
  53.6 34.4 %copy-start.70 = (f32[1792]{0:T(1024)}, f32[1792]{0:T(1024)S(1)}, u32[]{:S(2)}) copy-start(f32[1792]{0:T(1024)S(1)} %get-tuple-element.267) | copy-start | bytes 21508
  60.1 96.2 %copy-start.47 = (bf16[2,512,16]{1,2,0:T(8,128)(2,1)}, bf16[2,512,16]{1,2,0:T(8,128)(2,1)S(1)}, u32[]{:S(2)}) copy-start(bf16[2,512,16]{1,2,0:T(8,128)(2,1)S(1)} %convolution_convert_fusion.5) | copy-start | bytes 98308
  80.5 5.5 collective-permute-start
  116.2 365.4 %all-gather.18.cloned.1.call-start = ((), (), s32[]{:S(2)}) async-start(), calls=%async_computation.4 | async-start | bytes 3932160 | tf_op jit(solution)/shard_map/all_gather | solution.py:39
  140.2 49.8 %copy-start.78 = (f32[2,512]{1,0:T(2,128)}, f32[2,512]{1,0:T(2,128)S(1)}, u32[]{:S(2)}) copy-start(f32[2,512]{1,0:T(2,128)S(1)} %compare_convert_fusion) | copy-start | bytes 12292
  160.1 39.6 %copy-start.23 = (bf16[2,512,128]{2,1,0:T(8,128)(2,1)S(1)}, bf16[2,512,128]{2,1,0:T(8,128)(2,1)}, u32[]{:S(2)}) copy-start(bf16[2,512,128]{2,1,0:T(8,128)(2,1)} %copy-done.22) | copy-start | bytes 786436
  314.6 129.6 %copy-start.19 = (f32[2,1,24,64,128]{4,3,2,0,1:T(8,128)}, f32[2,1,24,64,128]{4,3,2,0,1:T(8,128)S(1)}, u32[]{:S(2)}) copy-start(f32[2,1,24,64,128]{4,3,2,0,1:T(8,128)S(1)} %fusion.55) | copy-start | bytes 4718596
  419.8 229.1 %all-reduce.13.cloned.1.call-start = ((), (), s32[]{:S(2)}) async-start(), calls=%async_computation.6 | async-start | bytes 25296896 | tf_op jit(solution)/shard_map/psum | solution.py:223
  567.0 12.5 %collective-permute-start.1 = (bf16[2,3,1792]{2,1,0:T(4,128)(2,1)S(1)}, bf16[2,3,1792]{2,1,0:T(4,128)(2,1)S(1)}, u32[]{:S(2)}, u32[]{:S(2)}) collective-permute-start(bf16[2,3,1792]{2,1,0:T(4,128)(2,1)S(1)} %slice.247), channel_id=1, source_target_pairs={{2,0},{4,2},{6,4},{3,1},{5,3},{7,5},{10,8},{12,10},{14,12},{11,9},... | collective-permute-start | bytes 64520 | tf_op jit(solution)/shard_map/ppermute | solution.py:17
  599.3 220.6 %all-reduce.11.cloned.1.call-start = ((), (), s32[]{:S(2)}) async-start(), calls=%async_computation.5 | async-start | bytes 7864320 | tf_op jit(solution)/shard_map/psum | solution.py:368
  605.1 43.7 %copy-start.4 = (bf16[2,512,1536]{2,1,0:T(8,128)(2,1)S(1)}, bf16[2,512,1536]{2,1,0:T(8,128)(2,1)}, u32[]{:S(2)}) copy-start(bf16[2,512,1536]{2,1,0:T(8,128)(2,1)} %param.28) | copy-start | bytes 9437188
  605.1 43.7 %copy-start.83 = (f32[1536]{0:T(1024)S(1)}, f32[1536]{0:T(1024)}, u32[]{:S(2)}) copy-start(f32[1536]{0:T(1024)} %param.32) | copy-start | bytes 18436
  605.2 43.7 %copy-start.90 = (f32[2,512]{1,0:T(2,128)S(1)}, f32[2,512]{1,0:T(2,128)}, u32[]{:S(2)}) copy-start(f32[2,512]{1,0:T(2,128)} %copy-done.89) | copy-start | bytes 12292
  611.4 41.0 %copy-start.58 = (bf16[2,1536,16]{1,0,2:T(2,128)(2,1)S(1)}, bf16[2,1536,16]{1,0,2:T(2,128)(2,1)}, u32[]{:S(2)}) copy-start(bf16[2,1536,16]{1,0,2:T(2,128)(2,1)} %convolution_convert_fusion.3) | copy-start | bytes 294916
  664.0 165.8 %copy-start.1 = (bf16[8,2,16,1536]{3,2,1,0:T(8,128)(2,1)S(1)}, bf16[8,2,16,1536]{3,2,1,0:T(8,128)(2,1)}, u32[]{:S(2)}) copy-start(bf16[8,2,16,1536]{3,2,1,0:T(8,128)(2,1)} %param.47) | copy-start | bytes 2359300
  (95 other events, 779.9 us)
Sparse Core Ops, SparseCore 0:
  9.9 62.4 all-gather.9
  74.2 56.9 all-gather.13
  133.0 56.9 all-gather.15
  192.0 115.3 all-gather.11
  419.9 61.6 all-gather.17
  599.4 49.4 all-reduce.12
  655.6 164.2 all-reduce.10
where the time goes:
time: 847 us; the launch traced here: 837 us
  waiting for transfers between devices  347 us (41%)
  matrix products  193 us (23%)
  local copies, waits for them, and re-layouts  112 us (13%)
  other arithmetic  108 us (13%)
  blocking collectives  55.3 us (7%)
  between operations  16 us (2%)
    psum x1, waiting for transfers between devices, on_device(): lax.psum((table_grads[0], table_grads[1], table_grads[2], table_grads[3])...  152 us
    all_gather x1, waiting for transfers between devices, carried_in(): pieces = jax.tree.map(lambda part: lax.all_gather(part, axis), value)  106 us
    psum x1, waiting for transfers between devices, on_device(): branch_total, low_total = lax.psum((partial_out, partial_low), 'tensor')  35.8 us
    all_gather x1, waiting for transfers between devices, on_device(): lax.all_gather(weights[4], 'dp', axis=0, tiled=True)  29.9 us
    unnamed x226, local copies, waits for them, and re-layouts  25.5 us
    reshape x2, local copies, waits for them, and re-layouts, on_device(): grad_x.reshape(slot_count, length, inner_width)  21 us
    reshape x2, local copies, waits for them, and re-layouts, on_device(): (inside + carried + head_skip_gain[:, None] * x_block.astype(jnp.float32)...  21 us
    mul x2, other arithmetic, on_device(): conv_weight[offset] * grad_conv  20.5 us
  transfers between devices with their start and end apart: 9, of which 6 were waited for; matrix products, arithmetic and copies ran while one was open for 22% of the time, Pallas kernels for 0%

commit v1 on v0

v1 whole, which is shorter than its diff:
```python
import functools

import jax
import jax.numpy as jnp
from jax import lax
from jax.experimental import pallas as pl
from jax.experimental.pallas import tpu as pltpu
from jax.sharding import PartitionSpec as P

MIXER_WIDTH = 3072
GROUP = 256
EPSILON = 1e-05
LANES = 128
HALO = 8
TURN = 8
F32 = jnp.float32
BF16 = jnp.bfloat16
VMEM_LIMIT = 60 * 1024 * 1024


def shifted(block, axis, distance):
    devices = range(lax.axis_size(axis))
    route = [(i - distance, i) for i in devices if i - distance in devices]
    return lax.ppermute(block, axis, route)


def partner(value, axis):
    size = lax.axis_size(axis)
    return lax.ppermute(value, axis, [(i, (i + 1) % size) for i in range(size)])


def swapped(value, axis, distance):
    return lax.ppermute(value, axis, [(i, i ^ distance) for i in range(lax.axis_size(axis))])


def rows_of_all(block):
    half = block.shape[0] // 2
    first, second = swapped(block, "dp", 1), swapped(block, "dp", 2)
    return block, first, second, swapped(first[:half], "dp", 2), swapped(second[half:], "dp", 1)


def dot(a, b):
    return jnp.dot(a, b, preferred_element_type=F32)


def dot_nt(a, b):
    return lax.dot_general(a, b, (((1,), (1,)), ((), ())), preferred_element_type=F32)


def dot_tn(a, b):
    return lax.dot_general(a, b, (((0,), (0,)), ((), ())), preferred_element_type=F32)


def split(value):
    high = value.astype(BF16)
    return high, (value - high.astype(F32)).astype(BF16)


def exact_dot(value, table):
    high, low = split(value)
    return dot(high, table) + dot(low, table)


def sigmoid(value):
    return 1.0 / (1.0 + jnp.exp(-value))


def silu_grad(value):
    g = sigmoid(value)
    return g * (1.0 + value * (1.0 - g))


def params(**more):
    return pltpu.CompilerParams(vmem_limit_bytes=VMEM_LIMIT, **more)


ANYWHERE = pl.BlockSpec(memory_space=pl.ANY)


def assemble(place, parts, table, sem):
    rows = parts[0].shape[0]
    half = rows // 2
    copies = []
    for step, first, part in zip((0, 1, 2, 3, 3), (0, 0, 0, 0, half), parts):
        at = pl.multiple_of((place ^ step) * rows + first, half)
        copies.append(pltpu.make_async_copy(part, table.at[pl.ds(at, part.shape[0])], sem))
    for copy in copies:
        copy.start()
    for copy in copies:
        copy.wait()


def whole(shape):
    return pl.BlockSpec(shape, lambda *_: (0,) * len(shape))


def running_sum(value, backwards=False):
    rows = value.shape[0]
    i = lax.broadcasted_iota(jnp.int32, (rows, rows), 0)
    j = lax.broadcasted_iota(jnp.int32, (rows, rows), 1)
    table = jnp.where(i <= j if backwards else i >= j, 1.0, 0.0).astype(F32)
    return jnp.dot(table, value, precision=lax.Precision.HIGHEST, preferred_element_type=F32)


def conv_taps(ext_ref, taps_ref, bias_ref, lanes, tap_count):
    value = jnp.zeros((GROUP, LANES), F32) + bias_ref[:, lanes]
    for k in range(tap_count):
        start = HALO - (tap_count - 1) + k
        value = value + taps_ref[k : k + 1, lanes] * ext_ref[start : start + GROUP, lanes]
    return value


def enter_kernel(
    tap_count, index_ref, tok_ref, halo_ref, gain_ref, w0, w1, w2, w3, w4, down_ref, up_ref, taps_ref,
    bias_ref, step_bias_ref, rate_ref, e_ref,
    normed_ref, low_ref, conv_ref, x_ref, bc_ref, raw_ref, cum_ref, loc_ref, before_ref, full_ref,
    ext, state, w_ref, sem, out_sem,
):
    b = pl.program_id(1)
    keep = pltpu.make_async_copy(w_ref, full_ref, out_sem)

    @pl.when((pl.program_id(0) == 0) & (b == 0))
    def _():
        assemble(index_ref[pl.num_programs(0)], (w0, w1, w2, w3, w4), w_ref, sem)
        keep.start()

    width = x_ref.shape[-1]
    conv_width = conv_ref.shape[-1]

    def project(tok):
        tok = tok.astype(F32)
        scale = lax.rsqrt(jnp.mean(tok * tok, axis=-1, keepdims=True) + EPSILON)
        normed = (tok * scale * gain_ref[...]).astype(BF16)
        low = dot(normed, down_ref[0]).astype(BF16)
        inner = dot(normed, w_ref[:, :width]) + dot(low, up_ref[0, 1])
        rest = dot(normed, w_ref[:, width:])
        return normed, low, inner, rest

    @pl.when(b == 0)
    def _():
        _, _, inner, rest = project(halo_ref[0])
        ext[:HALO, :width] = inner.astype(BF16).astype(F32)
        ext[:HALO, width:] = rest[:, : conv_width - width].astype(BF16).astype(F32)
        state[...] = jnp.zeros_like(state)

    @pl.when(b > 0)
    def _():
        ext[:HALO] = ext[GROUP:]

    before_ref[0, 0] = ext[:HALO].astype(BF16)
    normed, low, inner, rest = project(tok_ref[0])
    normed_ref[0] = normed
    low_ref[0] = low
    inner = inner.astype(BF16)
    states = rest[:, : conv_width - width].astype(BF16)
    conv_ref[0, :, :width] = inner
    conv_ref[0, :, width:] = states
    ext[HALO:, :width] = inner.astype(F32)
    ext[HALO:, width:] = states.astype(F32)
    raw = rest[:, conv_width - width :]
    raw_ref[0] = raw
    step = jax.nn.softplus(raw + step_bias_ref[...])
    cum = running_sum(step * rate_ref[...])
    cum_ref[0] = cum
    last = cum[GROUP - 1 :]
    tail = jnp.exp(last - cum) * step

    for at in range(width, conv_width, LANES):
        lanes = slice(at, at + LANES)
        value = conv_taps(ext, taps_ref, bias_ref, lanes, tap_count)
        bc_ref[0, :, at - width : at - width + LANES] = (value * sigmoid(value)).astype(BF16)
    b_mat = bc_ref[0, :, : bc_ref.shape[-1] // 2]
    tail_high, tail_low = split(tail)
    decay_high, decay_low = split(jnp.broadcast_to(jnp.exp(last), (HALO, LANES)))
    for at in range(0, width, LANES):
        lanes = slice(at, at + LANES)
        value = conv_taps(ext, taps_ref, bias_ref, lanes, tap_count)
        x = (value * sigmoid(value)).astype(BF16)
        x_ref[0, :, lanes] = x
        table = e_ref[:, lanes]
        weighted = (x.astype(F32) * (dot(tail_high, table) + dot(tail_low, table))).astype(BF16)
        decay = (dot(decay_high, table) + dot(decay_low, table))[:1]
        new = decay * state[:, lanes] + dot_tn(b_mat, weighted)
        state[:, lanes] = new
        loc_ref[0, 0, :, lanes] = new

    @pl.when((pl.program_id(0) == pl.num_programs(0) - 1) & (b == pl.num_programs(1) - 1))
    def _():
        keep.wait()


def enter(index, tokens, halo, gain, w, down, up, taps, bias, step_bias, rate, e, width, conv_width):
    s, length, model = tokens.shape
    blocks = length // GROUP
    rank = down.shape[-1]
    states = (conv_width - width) // 2
    rows = lambda n: pl.BlockSpec((1, GROUP, n), lambda i, j, _: (i, j, 0))
    out = lambda n, kind: jax.ShapeDtypeStruct((s, length, n), kind)
    return pl.pallas_call(
        functools.partial(enter_kernel, 4),
        grid_spec=pltpu.PrefetchScalarGridSpec(
            num_scalar_prefetch=1,
            grid=(s, blocks),
            in_specs=[
                rows(model),
                pl.BlockSpec((1, HALO, model), lambda i, j, _: (i, 0, 0)),
                whole(gain.shape),
                *[ANYWHERE] * 5,
                pl.BlockSpec((1, model, rank), lambda i, j, idx: (idx[i], 0, 0)),
                pl.BlockSpec((1, 2, rank, width), lambda i, j, idx: (idx[i], 0, 0, 0)),
                whole(taps.shape),
                whole(bias.shape),
                whole(step_bias.shape),
                whole(rate.shape),
                whole(e.shape),
            ],
            out_specs=[
                rows(model), rows(rank), rows(conv_width), rows(width), rows(2 * states),
                rows(LANES), rows(LANES),
                pl.BlockSpec((1, 1, states, width), lambda i, j, _: (i, j, 0, 0)),
                pl.BlockSpec((1, 1, HALO, conv_width), lambda i, j, _: (i, j, 0, 0)),
                ANYWHERE,
            ],
            scratch_shapes=[
                pltpu.VMEM((GROUP + HALO, conv_width), F32),
                pltpu.VMEM((states, width), F32),
                pltpu.VMEM((model, w[0].shape[1]), BF16),
                pltpu.SemaphoreType.DMA,
                pltpu.SemaphoreType.DMA,
            ],
        ),
        out_shape=[
            out(model, BF16), out(rank, BF16), out(conv_width, BF16), out(width, BF16),
            out(2 * states, BF16), out(LANES, F32), out(LANES, F32),
            jax.ShapeDtypeStruct((s, blocks, states, width), F32),
            jax.ShapeDtypeStruct((s, blocks, HALO, conv_width), BF16),
            jax.ShapeDtypeStruct((model, w[0].shape[1]), BF16),
        ],
        compiler_params=params(),
        name="enter",
        cost_estimate=pl.CostEstimate(flops=15_000_000_000, bytes_accessed=30_000_000, transcendentals=0),
    )(index, tokens, halo, gain, *w, down, up, taps, bias, step_bias, rate, e)


def inside_kernel(x_ref, bc_ref, raw_ref, cum_ref, step_bias_ref, skip_ref, y_ref, cum_t, step_t, scores):
    states = bc_ref.shape[-1] // 2
    heads_at = x_ref.shape[-1] // 64
    cum = cum_ref[0]
    step = jax.nn.softplus(raw_ref[0] + step_bias_ref[...])
    cum_t[...] = cum.T
    step_t[...] = step.T
    scores[...] = dot_nt(bc_ref[0, :, states:], bc_ref[0, :, :states])
    lane = lax.broadcasted_iota(jnp.int32, (GROUP, LANES), 1)
    causal = lax.broadcasted_iota(jnp.int32, (LANES, LANES), 0) >= lax.broadcasted_iota(
        jnp.int32, (LANES, LANES), 1
    )
    half = GROUP // 2

    @pl.loop(0, heads_at // TURN)
    def _(turn):
        rolled = pltpu.roll(cum, (LANES - TURN * turn) % LANES, 1)
        rows = pl.ds(pl.multiple_of(turn * TURN, TURN), TURN)
        cum_rows = cum_t[rows, :]
        step_rows = step_t[rows, :]
        for pair in range(TURN // 2):
            lanes = pl.ds(pl.multiple_of(turn * (TURN * 64) + pair * LANES, LANES), LANES)
            x = x_ref[0, :, lanes]
            top = skip_ref[:, lanes] * x[:half].astype(F32)
            bottom = skip_ref[:, lanes] * x[half:].astype(F32)
            for side in range(2):
                j = 2 * pair + side
                column = rolled[:, j : j + 1]
                cum_row = cum_rows[j : j + 1, :]
                step_row = step_rows[j : j + 1, :]
                own = jnp.where((lane < 64) == (side == 0), x, jnp.zeros_like(x))

                def mixing(r, c, masked):
                    diff = column[r] - cum_row[:, c]
                    if masked:
                        diff = jnp.where(causal, diff, -1e30)
                    return (scores[r, c] * jnp.exp(diff) * step_row[:, c]).astype(BF16)

                lo, hi = slice(0, half), slice(half, GROUP)
                top = top + dot(mixing(lo, lo, True), own[:half])
                bottom = bottom + dot(mixing(hi, lo, False), own[:half])
                bottom = bottom + dot(mixing(hi, hi, True), own[half:])
            y_ref[0, :half, lanes] = top
            y_ref[0, half:, lanes] = bottom


def inside(x, bc, raw, cum, step_bias, skip):
    s, length, width = x.shape
    rows = lambda n: pl.BlockSpec((1, GROUP, n), lambda i, j: (i, j, 0))
    return pl.pallas_call(
        inside_kernel,
        grid=(s, length // GROUP),
        in_specs=[
            rows(width), rows(bc.shape[-1]), rows(LANES), rows(LANES), whole(step_bias.shape),
            whole(skip.shape),
        ],
        out_specs=rows(width),
        out_shape=jax.ShapeDtypeStruct((s, length, width), F32),
        scratch_shapes=[
            pltpu.VMEM((LANES, GROUP), F32), pltpu.VMEM((LANES, GROUP), F32),
            pltpu.VMEM((GROUP, GROUP), F32),
        ],
        compiler_params=params(),
        name="inside",
        cost_estimate=pl.CostEstimate(flops=10_000_000_000, bytes_accessed=20_000_000, transcendentals=0),
    )(x, bc, raw, cum, step_bias, skip)


def product_kernel(
    rounded, index_ref, a_ref, w0, w1, w2, w3, w4, down_ref, up_ref, out_ref, full_ref, w_ref, sem, out_sem
):
    keep = pltpu.make_async_copy(w_ref, full_ref, out_sem)

    @pl.when((pl.program_id(0) == 0) & (pl.program_id(1) == 0))
    def _():
        assemble(index_ref[pl.num_programs(0)], (w0, w1, w2, w3, w4), w_ref, sem)
        keep.start()

    a = a_ref[0]
    up = up_ref[...].reshape(up_ref.shape[-2:]) if len(up_ref.shape) == 3 else up_ref[0, 0]
    if rounded:
        low = dot(a, down_ref[0]).astype(BF16)
        extra = dot(low, up)
    else:
        high, rest = split(dot_nt(a, down_ref[0]))
        extra = dot_nt(high, up) + dot_nt(rest, up)
    out_ref[0] = dot(a, w_ref[...]) + extra

    @pl.when((pl.program_id(0) == pl.num_programs(0) - 1) & (pl.program_id(1) == pl.num_programs(1) - 1))
    def _():
        keep.wait()


def product(index, a, w, down, up, rounded):
    s, length, depth = a.shape
    width = w[0].shape[1]
    tile = min(length, 2 * GROUP)
    down_spec = pl.BlockSpec((1,) + down.shape[1:], lambda i, j, idx: (idx[i], 0, 0))
    if rounded:
        up_spec = pl.BlockSpec((1, 1) + up.shape[2:], lambda i, j, idx: (idx[i], 0, 0, 0))
    else:
        up_spec = pl.BlockSpec((1,) + up.shape[1:], lambda i, j, idx: (idx[i], 0, 0))
    return pl.pallas_call(
        functools.partial(product_kernel, rounded),
        grid_spec=pltpu.PrefetchScalarGridSpec(
            num_scalar_prefetch=1,
            grid=(s, length // tile),
            in_specs=[
                pl.BlockSpec((1, tile, depth), lambda i, j, _: (i, j, 0)),
                *[ANYWHERE] * 5, down_spec, up_spec,
            ],
            out_specs=[pl.BlockSpec((1, tile, width), lambda i, j, _: (i, j, 0)), ANYWHERE],
            scratch_shapes=[
                pltpu.VMEM((depth, width), BF16), pltpu.SemaphoreType.DMA, pltpu.SemaphoreType.DMA,
            ],
        ),
        out_shape=[
            jax.ShapeDtypeStruct((s, length, width), F32), jax.ShapeDtypeStruct((depth, width), BF16)
        ],
        compiler_params=params(),
        name="product",
        cost_estimate=pl.CostEstimate(
            flops=2 * s * length * depth * width, bytes_accessed=15_000_000, transcendentals=0
        ),
    )(index, a, *w, down, up)


def gated_kernel(
    y_ref, bc_ref, cum_ref, loc_ref, in_ref, gate_ref, gn_ref, gain_ref, e_ref,
    mixer_ref, sums_ref, start_ref, entering,
):
    b = pl.program_id(1)
    states = bc_ref.shape[-1] // 2
    width = y_ref.shape[-1]
    cum = cum_ref[0]
    c_mat = bc_ref[0, :, states:]
    rise_high, rise_low = split(jnp.exp(cum))
    squares = jnp.zeros((GROUP, LANES), F32)
    crosses = jnp.zeros((GROUP, LANES), F32)

    for at in range(0, width, LANES):
        lanes = slice(at, at + LANES)
        table = e_ref[:, lanes]
        rise = dot(rise_high, table) + dot(rise_low, table)

        @pl.when(b == 0)
        def _():
            entering[:, lanes] = in_ref[0, :, lanes].astype(F32)

        own = jnp.where(b == 0, 0.0, loc_ref[0, 0, :, lanes])
        start = (entering[:, lanes] + own).astype(BF16)
        start_ref[0, 0, :, lanes] = start
        entering[:, lanes] = entering[:, lanes] * rise[GROUP - 1 :]
        mixer = y_ref[0, :, lanes] + dot(c_mat, start) * rise
        mixer_ref[0, :, lanes] = mixer
        gate = gate_ref[0, :, lanes]
        gated = mixer * (gate * sigmoid(gate))
        squares = squares + gated * gated
        crosses = crosses + gated * (gn_ref[0, :, lanes] * gain_ref[:, lanes])
    lane = lax.broadcasted_iota(jnp.int32, (GROUP, LANES), 1)
    square = jnp.sum(squares, axis=-1, keepdims=True)
    cross = jnp.sum(crosses, axis=-1, keepdims=True)
    both = jnp.where(lane == 0, square, jnp.where(lane == 1, cross, 0.0))
    sums_ref[0] = both.T[:HALO]


def gated(y, bc, cum, loc, came, gate, gn, gain, e):
    s, length, width = y.shape
    blocks = length // GROUP
    states = bc.shape[-1] // 2
    rows = lambda n: pl.BlockSpec((1, GROUP, n), lambda i, j: (i, j, 0))
    return pl.pallas_call(
        gated_kernel,
        grid=(s, blocks),
        in_specs=[
            rows(width), rows(2 * states), rows(LANES),
            pl.BlockSpec((1, 1, states, width), lambda i, j: (i, jnp.maximum(j - 1, 0), 0, 0)),
            pl.BlockSpec((1, states, width), lambda i, j: (i, 0, 0)),
            rows(width), rows(width), whole(gain.shape), whole(e.shape),
        ],
        out_specs=[
            rows(width),
            pl.BlockSpec((1, HALO, GROUP), lambda i, j: (i, 0, j)),
            pl.BlockSpec((1, 1, states, width), lambda i, j: (i, j, 0, 0)),
        ],
        out_shape=[
            jax.ShapeDtypeStruct((s, length, width), F32),
            jax.ShapeDtypeStruct((s, HALO, length), F32),
            jax.ShapeDtypeStruct((s, blocks, states, width), BF16),
        ],
        scratch_shapes=[pltpu.VMEM((states, width), F32)],
        compiler_params=params(),
        name="gated",
        cost_estimate=pl.CostEstimate(flops=500_000_000, bytes_accessed=30_000_000, transcendentals=0),
    )(y, bc, cum, loc, came, gate, gn, gain, e)


def turn_kernel(
    mixer_ref, gate_ref, gn_ref, sums_ref, other_ref, x_ref, bc_ref, cum_ref, start_ref, gain_ref,
    skip_ref, e_ref, et_ref,
    g_ref, gg_ref, nout_ref, fol_ref, pend_ref, gc_ref, row_ref, pending,
):
    j = pl.program_id(1)
    states = bc_ref.shape[-1] // 2
    width = x_ref.shape[-1]
    c_mat = bc_ref[0, :, states:]
    both = (sums_ref[0] + other_ref[0]).T
    scale = lax.rsqrt(both[:, 0:1] / MIXER_WIDTH + EPSILON)
    pull = scale * scale * scale * (both[:, 1:2] / MIXER_WIDTH)
    rise_high, rise_low = split(jnp.exp(cum_ref[0]))
    grad_c = jnp.zeros((GROUP, states), F32)
    row = jnp.zeros((GROUP, LANES), F32)
    for at in range(0, width, LANES):
        lanes = slice(at, at + LANES)
        table = e_ref[:, lanes]
        rise = dot(rise_high, table) + dot(rise_low, table)
        gate = gate_ref[0, :, lanes]
        mixer = mixer_ref[0, :, lanes]
        sig = sigmoid(gate)
        silu = gate * sig
        value = mixer * silu
        gain = gain_ref[:, lanes]
        nout_ref[0, :, lanes] = (value * scale * gain).astype(BF16)
        grad = scale * (gn_ref[0, :, lanes] * gain) - value * pull
        g = (grad * silu).astype(BF16)
        g_ref[0, :, lanes] = g
        gg_ref[0, :, lanes] = (grad * mixer * (sig * (1.0 + gate * (1.0 - sig)))).astype(BF16)
        gf = g.astype(F32)
        scaled = (gf * rise).astype(BF16)
        grad_c = grad_c + dot_nt(scaled, start_ref[0, 0, :, lanes])
        own = mixer - skip_ref[:, lanes] * x_ref[0, :, lanes].astype(F32)
        row = row + exact_dot(gf * own, et_ref[lanes, :])
        before = jnp.where(j == 0, 0.0, pending[:, lanes])
        fol_ref[0, 0, :, lanes] = before
        new = dot_tn(c_mat, scaled) + rise[GROUP - 1 :] * before
        pending[:, lanes] = new
        pend_ref[0, :, lanes] = new.astype(BF16)
    gc_ref[0] = grad_c
    row_ref[0] = row


def turn_back(mixer, gate, gn, sums, other, x, bc, cum, start, gain, skip, e, et):
    s, length, width = x.shape
    blocks = length // GROUP
    states = bc.shape[-1] // 2
    rows = lambda n: pl.BlockSpec((1, GROUP, n), lambda i, j: (i, blocks - 1 - j, 0))
    state = pl.BlockSpec((1, 1, states, width), lambda i, j: (i, blocks - 1 - j, 0, 0))
    sums_spec = pl.BlockSpec((1, HALO, GROUP), lambda i, j: (i, 0, blocks - 1 - j))
    out = lambda n, kind: jax.ShapeDtypeStruct((s, length, n), kind)
    return pl.pallas_call(
        turn_kernel,
        grid=(s, blocks),
        in_specs=[
            rows(width), rows(width), rows(width), sums_spec, sums_spec, rows(width),
            rows(2 * states), rows(LANES), state, whole(gain.shape), whole(skip.shape),
            whole(e.shape), whole(et.shape),
        ],
        out_specs=[
            rows(width), rows(width), rows(width), state,
            pl.BlockSpec((1, states, width), lambda i, j: (i, 0, 0)),
            rows(states), rows(LANES),
        ],
        out_shape=[
            out(width, BF16), out(width, BF16), out(width, BF16),
            jax.ShapeDtypeStruct((s, blocks, states, width), F32),
            jax.ShapeDtypeStruct((s, states, width), BF16),
            out(states, F32), out(LANES, F32),
        ],
        scratch_shapes=[pltpu.VMEM((states, width), F32)],
        compiler_params=params(),
        name="turn_back",
        cost_estimate=pl.CostEstimate(flops=2_000_000_000, bytes_accessed=35_000_000, transcendentals=0),
    )(mixer, gate, gn, sums, other, x, bc, cum, start, gain, skip, e, et)


def inside_back_kernel(
    x_ref, g_ref, bc_ref, raw_ref, cum_ref, step_bias_ref, et_ref,
    y_ref, gb_ref, gc_ref, direct_ref, cum_t, scores, grad_scores,
):
    states = bc_ref.shape[-1] // 2
    width = x_ref.shape[-1]
    cum = cum_ref[0]
    step = jax.nn.softplus(raw_ref[0] + step_bias_ref[...])
    cum_t[...] = cum.T
    b_mat = bc_ref[0, :, :states]
    c_mat = bc_ref[0, :, states:]
    scores[...] = dot_nt(b_mat, c_mat)
    grad_scores[...] = jnp.zeros_like(grad_scores)
    lane = lax.broadcasted_iota(jnp.int32, (GROUP, LANES), 1)
    causal = lax.broadcasted_iota(jnp.int32, (LANES, LANES), 0) <= lax.broadcasted_iota(
        jnp.int32, (LANES, LANES), 1
    )
    half = GROUP // 2
    direct_ref[0] = jnp.zeros((GROUP, LANES), F32)

    @pl.loop(0, width // 64 // TURN)
    def _(turn):
        shift = (LANES - TURN * turn) % LANES
        rolled = pltpu.roll(cum, shift, 1)
        rolled_step = pltpu.roll(step, shift, 1)
        cum_rows = cum_t[pl.ds(pl.multiple_of(turn * TURN, TURN), TURN), :]
        for pair in range(TURN // 2):
            at = pl.multiple_of(turn * (TURN * 64) + pair * LANES, LANES)
            lanes = pl.ds(at, LANES)
            x = x_ref[0, :, lanes]
            g = g_ref[0, :, lanes]
            top = jnp.zeros((half, LANES), F32)
            bottom = jnp.zeros((half, LANES), F32)
            for side in range(2):
                j = 2 * pair + side
                column = rolled[:, j : j + 1]
                step_column = rolled_step[:, j : j + 1]
                row = cum_rows[j : j + 1, :]
                own = jnp.where((lane < 64) == (side == 0), g, jnp.zeros_like(g))
                lo, hi = slice(0, half), slice(half, GROUP)

                def tile(r, c, masked):
                    diff = row[:, c] - column[r]
                    if masked:
                        diff = jnp.where(causal, diff, -1e30)
                    decay = jnp.exp(diff)
                    grad_mix = dot_nt(x[r], own[c])
                    grad_scores[r, c] += grad_mix * (decay * step_column[r])
                    return dot((scores[r, c] * decay).astype(BF16), own[c])

                top = top + tile(lo, lo, True) + tile(lo, hi, False)
                bottom = bottom + tile(hi, hi, True)
            y_ref[0, :half, lanes] = top
            y_ref[0, half:, lanes] = bottom
            et = et_ref[lanes, :]
            direct_ref[0, :half] += exact_dot(top * x[:half].astype(F32), et)
            direct_ref[0, half:] += exact_dot(bottom * x[half:].astype(F32), et)

    high, low = split(grad_scores[...])
    gb_ref[0] = dot(high, c_mat) + dot(low, c_mat)
    gc_ref[0] = dot_tn(high, b_mat) + dot_tn(low, b_mat)


def inside_back(x, g, bc, raw, cum, step_bias, et):
    s, length, width = x.shape
    states = bc.shape[-1] // 2
    rows = lambda n: pl.BlockSpec((1, GROUP, n), lambda i, j: (i, j, 0))
    out = lambda n: jax.ShapeDtypeStruct((s, length, n), F32)
    return pl.pallas_call(
        inside_back_kernel,
        grid=(s, length // GROUP),
        in_specs=[
            rows(width), rows(width), rows(2 * states), rows(LANES), rows(LANES),
            whole(step_bias.shape), whole(et.shape),
        ],
        out_specs=[rows(width), rows(states), rows(states), rows(LANES)],
        out_shape=[out(width), out(states), out(states), out(LANES)],
        scratch_shapes=[
            pltpu.VMEM((LANES, GROUP), F32), pltpu.VMEM((GROUP, GROUP), F32),
            pltpu.VMEM((GROUP, GROUP), F32),
        ],
        compiler_params=params(),
        name="inside_back",
        cost_estimate=pl.CostEstimate(flops=20_000_000_000, bytes_accessed=20_000_000, transcendentals=0),
    )(x, g, bc, raw, cum, step_bias, et)


def leave_kernel(
    tap_count, y_ref, x_ref, g_ref, bc_ref, raw_ref, cum_ref, conv_ref, before_ref, start_ref, fol_ref,
    later_ref, gb_ref, gc_ref, gc2_ref, row_ref, direct_ref, taps_ref, bias_ref, step_bias_ref,
    rate_ref, skip_ref, e_ref, et_ref,
    pack_ref, edge_ref, last_ref,
    ext, back, later,
):
    j = pl.program_id(1)
    width = x_ref.shape[-1]
    conv_width = conv_ref.shape[-1]
    states = (conv_width - width) // 2
    b_mat = bc_ref[0, :, :states]
    cum = cum_ref[0]
    raw = raw_ref[0] + step_bias_ref[...]
    step = jax.nn.softplus(raw)
    last = cum[GROUP - 1 :]
    fade = jnp.exp(last - cum)
    tail = fade * step
    tail_high, tail_low = split(tail)
    step_high, step_low = split(step)
    decay_high, decay_low = split(jnp.broadcast_to(jnp.exp(last), (HALO, LANES)))
    ext[:HALO] = before_ref[0, 0].astype(F32)
    ext[HALO:] = conv_ref[0].astype(F32)

    @pl.when(j == 0)
    def _():
        back[GROUP:] = jnp.zeros((HALO, conv_width), F32)

    @pl.when(j > 0)
    def _():
        back[GROUP:] = back[:HALO]

    grad_tail = jnp.zeros((GROUP, LANES), F32)
    grad_b = gb_ref[0]
    block_decay = jnp.zeros((HALO, LANES), F32)

    def through_conv(lanes, grad):
        value = conv_taps(ext, taps_ref, bias_ref, lanes, tap_count)
        back[:GROUP, lanes] = grad * silu_grad(value)
        total = jnp.zeros((GROUP, LANES), F32)
        for k in range(tap_count):
            ahead = tap_count - 1 - k
            total = total + taps_ref[k : k + 1, lanes] * back[ahead : ahead + GROUP, lanes]
        pack_ref[0, :, lanes] = total.astype(BF16)
        last_ref[0, :, lanes] = jnp.where(j == 0, total[GROUP - HALO :], last_ref[0, :, lanes])

    for at in range(0, width, LANES):
        lanes = slice(at, at + LANES)
        table = e_ref[:, lanes]
        et = et_ref[lanes, :]

        @pl.when(j == 0)
        def _():
            later[:, lanes] = later_ref[0, :, lanes].astype(F32)

        x = x_ref[0, :, lanes].astype(F32)
        whole_grad = later[:, lanes] + fol_ref[0, 0, :, lanes]
        fresh = whole_grad.astype(BF16)
        start = start_ref[0, 0, :, lanes].astype(F32)
        decay = (dot(decay_high, table) + dot(decay_low, table))[:1]
        later[:, lanes] = later[:, lanes] * decay
        product = jnp.sum(whole_grad * start, axis=0, keepdims=True)
        block_decay = block_decay + exact_dot(jnp.broadcast_to(product, (HALO, LANES)), et)
        tails = dot(tail_high, table) + dot(tail_low, table)
        steps = dot(step_high, table) + dot(step_low, table)
        by_b = dot(b_mat, fresh)
        weighted = (x * tails).astype(BF16)
        grad_b = grad_b + dot_nt(weighted, fresh)
        grad_tail = grad_tail + exact_dot(by_b * x, et)
        grad_x = (
            steps * y_ref[0, :, lanes]
            + skip_ref[:, lanes] * g_ref[0, :, lanes].astype(F32)
            + by_b * tails
        )
        through_conv(lanes, grad_x)
    through_conv(slice(width, width + states), grad_b)
    through_conv(slice(width + states, conv_width), gc_ref[0] + gc2_ref[0])

    direct = direct_ref[0]
    tail_pull = grad_tail * tail
    end_pull = jnp.sum(tail_pull, axis=0, keepdims=True) + block_decay[:1] * jnp.exp(last)
    at_end = lax.broadcasted_iota(jnp.int32, (GROUP, LANES), 0) == GROUP - 1
    grad_cum = row_ref[0] - step * direct - tail_pull + jnp.where(at_end, end_pull, 0.0)
    grad_step = direct + grad_tail * fade + running_sum(grad_cum, True) * rate_ref[...]
    lane = lax.broadcasted_iota(jnp.int32, (GROUP, LANES), 1)
    grad_raw = jnp.where(lane < width // 64, grad_step * sigmoid(raw), 0.0)
    pack_ref[0, :, conv_width:] = grad_raw.astype(BF16)

    rows = []
    for position in range(-HALO, 0):
        total = jnp.zeros((1, conv_width), F32)
        for k in range(tap_count):
            at = position + tap_count - 1 - k
            if at >= 0:
                total = total + taps_ref[k : k + 1, :] * back[at : at + 1, :]
        rows.append(total)
    edge_ref[0] = jnp.concatenate(rows, axis=0)


def leave(
    y, x, g, bc, raw, cum, conv, before, start, fol, later, gb, gc, gc2, row, direct, taps, bias,
    step_bias, rate, skip, e, et,
):
    s, length, width = x.shape
    conv_width = conv.shape[-1]
    blocks = length // GROUP
    states = bc.shape[-1] // 2
    rows = lambda n: pl.BlockSpec((1, GROUP, n), lambda i, j: (i, blocks - 1 - j, 0))
    state = pl.BlockSpec((1, 1, states, width), lambda i, j: (i, blocks - 1 - j, 0, 0))
    edge = pl.BlockSpec((1, HALO, conv_width), lambda i, j: (i, 0, 0))
    return pl.pallas_call(
        functools.partial(leave_kernel, 4),
        grid=(s, blocks),
        in_specs=[
            rows(width), rows(width), rows(width), rows(2 * states), rows(LANES), rows(LANES),
            rows(conv_width),
            pl.BlockSpec((1, 1, HALO, conv_width), lambda i, j: (i, blocks - 1 - j, 0, 0)),
            state, state, pl.BlockSpec((1, states, width), lambda i, j: (i, 0, 0)),
            rows(states), rows(states), rows(states), rows(LANES), rows(LANES),
            whole(taps.shape), whole(bias.shape), whole(step_bias.shape), whole(rate.shape),
            whole(skip.shape), whole(e.shape), whole(et.shape),
        ],
        out_specs=[rows(conv_width + LANES), edge, edge],
        out_shape=[
            jax.ShapeDtypeStruct((s, length, conv_width + LANES), BF16),
            jax.ShapeDtypeStruct((s, HALO, conv_width), F32),
            jax.ShapeDtypeStruct((s, HALO, conv_width), F32),
        ],
        scratch_shapes=[
            pltpu.VMEM((GROUP + HALO, conv_width), F32),
            pltpu.VMEM((GROUP + HALO, conv_width), F32),
            pltpu.VMEM((states, width), F32),
        ],
        compiler_params=params(),
        name="leave",
        cost_estimate=pl.CostEstimate(flops=2_000_000_000, bytes_accessed=40_000_000, transcendentals=0),
    )(
        y, x, g, bc, raw, cum, conv, before, start, fol, later, gb, gc, gc2, row, direct, taps, bias,
        step_bias, rate, skip, e, et,
    )


def chained(decay, own, axis, distance):
    leaving = own
    for _ in range(lax.axis_size(axis) - 1):
        came = shifted(leaving.astype(BF16), axis, distance)
        leaving = decay * came.astype(F32) + own
    return came


def by_adapter(per_slot, everyone):
    distance = 1
    while distance < lax.axis_size("ctx"):
        mine = per_slot.astype(BF16)
        per_slot = mine.astype(F32) + swapped(mine, "ctx", distance).astype(F32)
        distance *= 2
    slots = per_slot.astype(BF16)
    for distance in (1, 2):
        slots = jnp.concatenate([slots, swapped(slots, "dp", distance)])
    return jnp.einsum("sa,src->arc", everyone, slots, preferred_element_type=F32)


def partner_sum(value, kind):
    mine = value.astype(kind)
    return mine.astype(F32) + partner(mine, "tensor").astype(F32)


def on_device(
    tokens,
    cotangent,
    lengths,
    slot_adapter_index,
    input_norm_gain,
    gate_weight_matrix,
    inner_weight_matrix,
    state_map_weight,
    step_size_weight,
    output_projection_weight,
    inner_channel_taps,
    state_map_taps,
    inner_conv_bias,
    state_map_conv_bias,
    step_size_bias,
    log_decay_rate,
    head_skip_gain,
    gated_norm_gain,
    adapter_in_down_maps,
    adapter_in_up_maps,
    adapter_out_down_maps,
    adapter_out_up_maps,
):
    slot_count, length, model_width = tokens.shape
    width = gate_weight_matrix.shape[1]
    heads = step_size_bias.shape[0]
    head_dim = width // heads
    conv_width = width + state_map_weight.shape[1]
    taps_before = inner_channel_taps.shape[0] - 1
    adapter_set = adapter_in_down_maps.shape[0]
    rank = adapter_in_down_maps.shape[-1]
    spare = -heads % LANES
    rows = step_size_weight.shape[0]
    picks = jnp.broadcast_to(slot_adapter_index.astype(BF16)[None], (rows, slot_count))
    packed = jnp.concatenate(
        [
            inner_weight_matrix,
            state_map_weight,
            step_size_weight,
            jnp.zeros((rows, spare - slot_count), BF16),
            picks,
        ],
        axis=1,
    )
    halo = shifted(tokens[:, length - HALO :], "ctx", 1)
    packed_parts = rows_of_all(packed)
    out_mine, packed_parts = lax.optimization_barrier((output_projection_weight, packed_parts))
    out_parts = rows_of_all(out_mine)
    gate_mine, *arrived = lax.optimization_barrier((gate_weight_matrix, *out_parts[1:3]))
    out_parts = (out_parts[0], *arrived, *out_parts[3:])
    gate_parts = rows_of_all(gate_mine)
    all_slots = jnp.concatenate([part[0, -slot_count:] for part in packed_parts[:4]])
    everyone = (all_slots[:, None] == jnp.arange(adapter_set, dtype=jnp.int32).astype(BF16)[None, :]).astype(BF16)
    index = jnp.concatenate([slot_adapter_index, lax.axis_index("dp")[None].astype(jnp.int32)])
    places = lax.axis_index("ctx") * length + jnp.arange(length, dtype=jnp.int32)
    live_mask = (places[None, :] < lengths[:, None]).astype(F32)[..., None]
    selector = (
        slot_adapter_index[:, None] == jnp.arange(adapter_set, dtype=jnp.int32)[None, :]
    ).astype(BF16)

    head_of = jnp.arange(width, dtype=jnp.int32) // head_dim
    e = (jnp.arange(LANES, dtype=jnp.int32)[:, None] == head_of[None, :]).astype(BF16)
    et = (head_of[:, None] == jnp.arange(LANES, dtype=jnp.int32)[None, :]).astype(BF16)
    step_bias = jnp.pad(step_size_bias, (0, spare))[None]
    rate = jnp.pad(-jnp.exp(log_decay_rate), (0, spare))[None]
    skip = jnp.repeat(head_skip_gain, head_dim)[None]
    gain = gated_norm_gain[None]
    taps = jnp.concatenate([inner_channel_taps, state_map_taps], axis=1)
    conv_bias = jnp.concatenate([inner_conv_bias, state_map_conv_bias])[None]
    grad_branch = (cotangent.astype(F32) * live_mask).astype(BF16)

    normed, low_in, conv, x, bc, raw, cum, loc, before, packed_full = enter(
        index, tokens, halo, input_norm_gain[None], packed_parts, adapter_in_down_maps,
        adapter_in_up_maps, taps, conv_bias, step_bias, rate, e, width, conv_width,
    )
    device_decay = jnp.exp(jnp.sum(cum[:, GROUP - 1 :: GROUP, :heads], axis=1))
    device_decay = jnp.repeat(device_decay, head_dim, axis=1)[:, None, :]
    came = chained(device_decay, loc[:, -1], "ctx", 1)
    y = inside(x, bc, raw, cum, step_bias, skip)
    grad_normed, out_full = product(
        index, grad_branch, out_parts, adapter_out_up_maps, adapter_out_down_maps, False
    )
    gate, gate_full = product(index, normed, gate_parts, adapter_in_down_maps, adapter_in_up_maps, True)
    mixer, sums, start = gated(y, bc, cum, loc, came, gate, grad_normed, gain, e)
    other = partner(sums, "tensor")
    g, grad_gate, normed_out, fol, pend, grad_c2, row = turn_back(
        mixer, gate, grad_normed, sums, other, x, bc, cum, start, gain, skip, e, et
    )
    later = chained(device_decay, pend.astype(F32), "ctx", -1)

    out_down = jnp.einsum("sa,acr->scr", selector, adapter_out_down_maps, preferred_element_type=F32)
    out_down = out_down.astype(BF16)
    out_up = jnp.einsum("sa,ard->srd", selector, adapter_out_up_maps, preferred_element_type=F32)
    out_up = out_up.astype(BF16)
    partial_low = jnp.einsum("stc,scr->str", normed_out, out_down, preferred_element_type=F32)
    low_out = partner_sum(partial_low, F32).astype(BF16)
    partial_out = jnp.stack(
        [
            partner_sum(
                lax.dot_general(normed_out[s], out_full, (((1,), (1,)), ((), ())), preferred_element_type=F32),
                BF16,
            )
            for s in range(slot_count)
        ]
    )
    branch = partial_out + jnp.einsum("str,srd->std", low_out, out_up, preferred_element_type=F32)
    result = (tokens.astype(F32) + live_mask * branch).astype(BF16)
    grad_low_out = jnp.einsum("std,srd->str", grad_branch, out_up, preferred_element_type=F32)
    up_out_grad = jnp.einsum("str,std->srd", low_out, grad_branch, preferred_element_type=F32)
    down_out_grad = jnp.einsum(
        "str,stc->src", grad_low_out, normed_out.astype(F32), precision=lax.Precision.HIGH
    )
    in_down = jnp.einsum("sa,adr->sdr", selector, adapter_in_down_maps, preferred_element_type=F32)
    in_up = jnp.einsum("sa,aqrc->sqrc", selector, adapter_in_up_maps, preferred_element_type=F32)
    in_up = in_up.astype(BF16)
    up_gate_grad = jnp.einsum("str,stc->src", low_in, grad_gate, preferred_element_type=F32)
    early = by_adapter(jnp.concatenate([up_out_grad, down_out_grad, up_gate_grad], axis=1), everyone)
    nt = (((1,), (1,)), ((), ()))
    gate_low = jnp.einsum("stc,src->str", grad_gate, in_up[:, 0], preferred_element_type=F32)
    gate_in = [
        lax.dot_general(grad_gate[s], gate_full, nt, preferred_element_type=F32) for s in range(slot_count)
    ]
    gate_low, gate_in, later = lax.optimization_barrier((gate_low, gate_in, later))

    y_back, grad_b, grad_c, direct = inside_back(x, g, bc, raw, cum, step_bias, et)
    pack, edge, last = leave(
        y_back, x, g, bc, raw, cum, conv, before, start, fol, later, grad_b, grad_c, grad_c2, row,
        direct, taps, conv_bias, step_bias, rate, skip, e, et,
    )
    edge = shifted(edge[:, HALO - taps_before :].astype(BF16), "ctx", -1).astype(F32)
    last = last + jnp.pad(edge, ((0, 0), (HALO - taps_before, 0), (0, 0)))
    pack = lax.dynamic_update_slice(pack, last.astype(BF16), (0, length - HALO, 0))
    up_wide = jnp.pad(in_up[:, 1], ((0, 0), (0, 0), (0, pack.shape[-1] - width)))
    grad_low_sum = partner_sum(
        gate_low + jnp.einsum("stc,src->str", pack, up_wide, preferred_element_type=F32), F32
    )
    up_inner_grad = jnp.einsum("str,stc->src", low_in, pack, preferred_element_type=F32)[..., :width]
    down_in_grad = jnp.einsum(
        "str,std->srd", grad_low_sum, normed.astype(F32), precision=lax.Precision.HIGH
    )
    late = by_adapter(jnp.concatenate([up_inner_grad, down_in_grad], axis=1), everyone)
    partial_in = jnp.stack(
        [
            partner_sum(
                gate_in[s] + lax.dot_general(pack[s], packed_full, nt, preferred_element_type=F32), BF16
            )
            for s in range(slot_count)
        ]
    )
    grad_normed_in = partial_in + jnp.einsum(
        "str,sdr->std", grad_low_sum, in_down, precision=lax.Precision.HIGH
    )
    tok = tokens.astype(F32)
    in_scale = lax.rsqrt(jnp.mean(tok * tok, axis=-1, keepdims=True) + EPSILON)
    weighted = grad_normed_in * input_norm_gain
    grad_tokens = (
        cotangent.astype(F32)
        + in_scale * weighted
        - tok * in_scale**3 * jnp.mean(tok * weighted, axis=-1, keepdims=True)
    )
    return (
        result,
        grad_tokens,
        late[:, rank:].transpose(0, 2, 1),
        jnp.stack([early[:, 2 * rank :], late[:, :rank]], axis=1),
        early[:, rank : 2 * rank].transpose(0, 2, 1),
        early[:, :rank],
    )


def solution(mesh):
    in_specs = (
        P("dp", "ctx", None),
        P("dp", "ctx", None),
        P("dp"),
        P("dp"),
        P(),
        P("dp", "tensor"),
        P("dp", "tensor"),
        P("dp", None),
        P("dp", "tensor"),
        P("dp", "tensor"),
        P(None, "tensor"),
        P(),
        P("tensor"),
        P(),
        P("tensor"),
        P("tensor"),
        P("tensor"),
        P("tensor"),
        P(),
        P(None, None, None, "tensor"),
        P(None, "tensor", None),
        P(),
    )
    out_specs = (
        P("dp", "ctx", None),
        P("dp", "ctx", None),
        P(),
        P(None, None, None, "tensor"),
        P(None, "tensor", None),
        P(),
    )
    return jax.shard_map(
        on_device, mesh=mesh, in_specs=in_specs, out_specs=out_specs, check_vma=False
    )
```

time: 847 us -> 456 us (0.54)
  waiting for transfers between devices: 347 us -> 94.3 us
  Pallas kernels: 0 us -> 163 us
  matrix products: 193 us -> 59.3 us
  other arithmetic: 108 us -> 29.6 us
  local copies, waits for them, and re-layouts: 112 us -> 47.2 us
  blocking collectives: 55.3 us -> 0 us
  starting transfers between devices: 5.56 us -> 52.4 us
  between operations: 16 us -> 1.89 us
    psum x2 -> x0, waiting for transfers between devices: 188 us -> none  [the longest x1 152 us: on_device(): lax.psum((table_grads[0], table_grads[1], table_grads[2], table_grads[3])...]
    pallas_call x0 -> x8, Pallas kernels: none -> 163 us  [the longest x1 31.1 us: leave(): pl.pallas_call(functools.partial(leave_kernel, 4), grid=(s, blocks), in_s...]
    all_gather x5 -> x0, waiting for transfers between devices: 156 us -> none  [the longest x1 106 us: carried_in(): pieces = jax.tree.map(lambda part: lax.all_gather(part, axis), value)]
    dot_general x44 -> x22, matrix products: 192 us -> 58.4 us  [the longest x2 13.2 us: on_device(): lax.dot_general(grad_gate[s], gate_full, nt, preferred_element_type=F32)]
    ppermute x0 -> x27, waiting for transfers between devices: none -> 75.1 us  [the longest x20 73.9 us: swapped(): lax.ppermute(value, axis, [(i, i ^ distance) for i in range(lax.axis_size...]
    reshape x11 -> x0, local copies, waits for them, and re-layouts: 70.1 us -> none  [the longest x2 21 us: on_device(): grad_x.reshape(slot_count, length, inner_width)]
    all_gather x4 -> x0, blocking collectives: 48 us -> none  [the longest x1 18.9 us: on_device(): lax.all_gather(weights[2], 'dp', axis=0, tiled=True)]
    mul x8 -> x0, other arithmetic: 31.3 us -> none  [the longest x2 20.5 us: on_device(): conv_weight[offset] * grad_conv]
  transfers between devices with their start and end apart: 9 -> 35, of which waited for: 6 -> 16; matrix products, arithmetic and copies ran while one was open for 22% -> 22% of each run, Pallas kernels for 0% -> 21%
where the time goes in v1:
time: 456 us; the launch traced here: 447 us
  Pallas kernels  163 us (36%)
  waiting for transfers between devices  94.3 us (21%)
  matrix products  59.3 us (13%)
  starting transfers between devices  52.4 us (11%)
  local copies, waits for them, and re-layouts  47.2 us (10%)
  other arithmetic  29.6 us (6%)
    ppermute x20, waiting for transfers between devices, swapped(): lax.ppermute(value, axis, [(i, i ^ distance) for i in range(lax.axis_size...  73.9 us
    pallas_call x1, Pallas kernels, leave(): pl.pallas_call(functools.partial(leave_kernel, 4), grid=(s, blocks), in_s...  31.1 us
    pallas_call x1, Pallas kernels, enter(): pl.pallas_call(functools.partial(enter_kernel, 4), grid_spec=pltpu.Prefet...  30.4 us
    ppermute x20, starting transfers between devices, swapped(): lax.ppermute(value, axis, [(i, i ^ distance) for i in range(lax.axis_size...  29.1 us
    pallas_call x2, Pallas kernels, product(): pl.pallas_call(functools.partial(product_kernel, rounded), grid_spec=pltp...  28.9 us
    pallas_call x1, Pallas kernels, inside_back(): pl.pallas_call(inside_back_kernel, grid=(s, length // GROUP), in_specs=[r...  23.9 us
    ppermute x8, starting transfers between devices, shifted(): return lax.ppermute(block, axis, route)  22.3 us
    unnamed x117, local copies, waits for them, and re-layouts  21.2 us
  transfers between devices with their start and end apart: 35, of which 16 were waited for; matrix products, arithmetic and copies ran while one was open for 22% of the time, Pallas kernels for 21%

profile of v1, /device:TPU:0, one launch (start us, length us, event | category | flops | bytes accessed | tf_op | source)
XLA Modules:
  0.0 447.3 jit_solution(16099403297111220061)
XLA Ops:
  29.0 14.5 %collective-permute-done.2.w2 = bf16[384,1920]{1,0:T(8,128)(2,1)} collective-permute-done((bf16[384,1920]{1,0:T(8,128)(2,1)}, bf16[384,1920]{1,0:T(8,128)(2,1)}, u32[]{:S(2)}, u32[]{:S(2)}) %collective-permute-start.2) | collective-permute-done | bytes 1474592 | tf_op jit(solution)/shard_map/ppermute | solution.py:33
  55.2 7.3 %collective-permute-done.4.w4 = bf16[192,1920]{1,0:T(8,128)(2,1)S(1)} collective-permute-done((bf16[192,1920]{1,0:T(8,128)(2,1)S(1)}, bf16[192,1920]{1,0:T(8,128)(2,1)S(1)}, u32[]{:S(2)}, u32[]{:S(2)}) %collective-permute-start.4) | collective-permute-done | bytes 737312 | tf_op jit(solution)/shard_map/ppermute | solution.py:33
  66.9 30.4 %enter.1 = (bf16[2,512,1536]{2,1,0:T(8,128)(2,1)}, bf16[2,512,16]{2,1,0:T(8,128)(2,1)}, bf16[2,512,1792]{2,1,0:T(8,128)(2,1)}, bf16[2,512,1536]{2,1,0:T(8,128)(2...) custom-call(s32[3]{0:T(128)} %pad_add_fusion.index_ref, ...), custom_call_target="tpu_custom_call" | custom-call | flops 15000000512 | bytes 30000000 | tf_op jit(solution)/shard_map/enter/pallas_call | solution.py:199
  120.1 5.5 %collective-permute-start.6 = (bf16[2,128,1536]{2,1,0:T(8,128)(2,1)}, bf16[2,128,1536]{2,1,0:T(8,128)(2,1)}, u32[]{:S(2)}, u32[]{:S(2)}) collective-permute-start(bf16[2,128,1536]{2,1,0:T(8,128)(2,1)} %add_convert_fusion.3), channel_id=1, source_target_pairs={{0,2},{2,4},{4,6},{1,3},{3,5},{5,7},{8,10},{10,12},{12,14},{9,11},... | collective-permute-start | bytes 2359304 | tf_op jit(solution)/shard_map/ppermute | solution.py:24
  127.7 11.8 %inside.1.y_ref = f32[2,512,1536]{2,1,0:T(8,128)} custom-call(bf16[2,512,1536]{2,1,0:T(8,128)(2,1)} %get-tuple-element.55.x_ref, bf16[2,512,256]{2,1,0:T(8,128)(2,1)} %get-tuple-element.56.bc_ref, f32[2,512,128]{2,1,0:T(8,128)} %get-tuple-element.57.raw_ref, f32[2,512,128]{2,1,0:T(8,128)} %get-tuple-element.58.cum_ref, ...), custom_call_target="tpu_custom_call" | custom-call | flops 10000000000 | bytes 20000000 | tf_op jit(solution)/shard_map/inside/pallas_call | solution.py:294
  145.4 9.5 %collective-permute-done.11.w2 = bf16[384,1536]{1,0:T(8,128)(2,1)} collective-permute-done((bf16[384,1536]{1,0:T(8,128)(2,1)}, bf16[384,1536]{1,0:T(8,128)(2,1)}, u32[]{:S(2)}, u32[]{:S(2)}) %collective-permute-start.11) | collective-permute-done | bytes 1179680 | tf_op jit(solution)/shard_map/ppermute | solution.py:33
  169.1 14.0 %product.3 = (f32[2,512,1536]{2,1,0:T(8,128)}, bf16[1536,1536]{1,0:T(8,128)(2,1)}) custom-call(s32[3]{0:T(128)} %pad_add_fusion.index_ref, bf16[2,512,1536]{2,1,0:T(8,128)(2,1)} %copy-done.1, bf16[384,1536]{1,0:T(8,128)(2,1)} %w0.1, bf16[384,1536]{1,0:T(8,128)(2,1)} %collective-permute-done.8.w1, bf16[384,1536]{1,0:T(8,128)(2,1)} %collective-permute-done.9.w2, ...), custom_call_target="tpu_custom_call" | custom-call | flops 4831838208 | bytes 15000000 | tf_op jit(solution)/shard_map/product/pallas_call | solution.py:347
  183.1 14.9 %product.2 = (f32[2,512,1536]{2,1,0:T(8,128)}, bf16[1536,1536]{1,0:T(8,128)(2,1)}) custom-call(s32[3]{0:T(128)} %pad_add_fusion.index_ref, bf16[2,512,1536]{2,1,0:T(8,128)(2,1)} %get-tuple-element.60.a_ref, bf16[384,1536]{1,0:T(8,128)(2,1)} %w0, bf16[384,1536]{1,0:T(8,128)(2,1)} %collective-permute-done.10.w1, bf16[384,1536]{1,0:T(8,128)(2,1)} %collective-permute-done.11.w2, ...), custom_call_target="tpu_custom_call" | custom-call | flops 4831838208 | bytes 15000000 | tf_op jit(solution)/shard_map/product/pallas_call | solution.py:347
  198.9 17.6 %gated.1 = (f32[2,512,1536]{2,1,0:T(8,128)}, f32[2,8,512]{2,1,0:T(8,128)}, bf16[2,2,128,1536]{3,2,1,0:T(8,128)(2,1)}) custom-call(f32[2,512,1536]{2,1,0:T(8,128)} %inside.1.y_ref, bf16[2,512,256]{2,1,0:T(8,128)(2,1)} %get-tuple-element.56.bc_ref, f32[2,512,128]{2,1,0:T(8,128)} %get-tuple-element.58.cum_ref, f32[2,2,128,1536]{3,2,1,0:T(8,128)} %get-tuple-element.59.loc_ref, ...), custom_call_target="tpu_custom_call" | custom-call | flops 500000000 | bytes 30000000 | tf_op jit(solution)/shard_map/gated/pallas_call | solution.py:416
  218.6 18.9 %turn_back.1 = (bf16[2,512,1536]{2,1,0:T(8,128)(2,1)}, bf16[2,512,1536]{2,1,0:T(8,128)(2,1)}, bf16[2,512,1536]{2,1,0:T(8,128)(2,1)}, f32[2,2,128,1536]{3,2,1,0:T...) custom-call(f32[2,512,1536]{2,1,0:T(8,128)} %get-tuple-element.67.mixer_ref, ...), custom_call_target="tpu_custom_call" | custom-call | flops 2000000000 | bytes 35000000 | tf_op jit(solution)/shard_map/turn_back/pallas_call | solution.py:494
  237.6 6.8 %convolution_convert_fusion = bf16[512,1536]{1,0:T(8,128)(2,1)} fusion(bf16[1536,1536]{1,0:T(8,128)(2,1)} %get-tuple-element.71, bf16[2,512,1536]{2,1,0:T(8,128)(2,1)} %get-tuple-element.70), kind=kOutput, calls=%fused_computation.22 | convolution fusion | flops 2416705536 | bytes 7864320 | tf_op jit(solution)/shard_map/dot_general | solution.py:874
  244.4 6.2 %convolution_convert_fusion.1 = bf16[512,1536]{1,0:T(8,128)(2,1)} fusion(bf16[1536,1536]{1,0:T(8,128)(2,1)} %get-tuple-element.71, bf16[2,512,1536]{2,1,0:T(8,128)(2,1)S(1)} %copy-done.8), kind=kOutput, calls=%fused_computation.23 | convolution fusion | flops 2416705536 | bytes 7864320 | tf_op jit(solution)/shard_map/dot_general | solution.py:874
  259.8 23.9 %inside_back.1 = (f32[2,512,1536]{2,1,0:T(8,128)}, f32[2,512,128]{2,1,0:T(8,128)}, f32[2,512,128]{2,1,0:T(8,128)}, f32[2,512,128]{2,1,0:T(8,128)}) custom-call(bf16[2,512,1536]{2,1,0:T(8,128)(2,1)} %get-tuple-element.55.x_ref, bf16[2,512,1536]{2,1,0:T(8,128)(2,1)} %get-tuple-element.76.g_ref, bf16[2,512,256]{2,1,0:T(8,128)(2,1)} %get-tuple-element.56.bc_ref, ...), custom_call_target="tpu_custom_call" | custom-call | flops 20000000000 | bytes 20000000 | tf_op jit(solution)/shard_map/inside_back/pallas_call | solution.py:588
  287.3 6.6 %fusion.12 = f32[512,1536]{1,0:T(8,128)} fusion(bf16[1536,1536]{1,0:T(8,128)(2,1)} %get-tuple-element.73, bf16[2,512,1536]{2,1,0:T(8,128)(2,1)S(1)} %copy-done.7), kind=kOutput, calls=%fused_computation.40 | convolution fusion | flops 2415919104 | bytes 9437184 | tf_op jit(solution)/shard_map/dot_general | solution.py:895
  293.9 6.5 %collective-permute-done.32 = bf16[2,48,1536]{2,1,0:T(8,128)(2,1)S(1)} collective-permute-done((bf16[2,48,1536]{2,1,0:T(8,128)(2,1)S(1)}, bf16[2,48,1536]{2,1,0:T(8,128)(2,1)S(1)}, u32[]{:S(2)}, u32[]{:S(2)}) %collective-permute-start.32) | collective-permute-done | bytes 294944 | tf_op jit(solution)/shard_map/ppermute | solution.py:33
  301.8 6.6 %fusion.14 = f32[512,1536]{1,0:T(8,128)} fusion(bf16[1536,1536]{1,0:T(8,128)(2,1)} %get-tuple-element.73, bf16[2,512,1536]{2,1,0:T(8,128)(2,1)S(1)} %copy-done.7), kind=kOutput, calls=%fused_computation.42 | convolution fusion | flops 2415919104 | bytes 9437184 | tf_op jit(solution)/shard_map/dot_general | solution.py:895
  314.7 9.4 %collective-permute-done.34 = bf16[4,48,1536]{2,1,0:T(8,128)(2,1)S(1)} collective-permute-done((bf16[4,48,1536]{2,1,0:T(8,128)(2,1)S(1)}, bf16[4,48,1536]{2,1,0:T(8,128)(2,1)S(1)}, u32[]{:S(2)}, u32[]{:S(2)}) %collective-permute-start.34) | collective-permute-done | bytes 589856 | tf_op jit(solution)/shard_map/ppermute | solution.py:33
  327.9 5.6 %collective-permute-done.21 = bf16[2,128,1536]{2,1,0:T(8,128)(2,1)S(1)} collective-permute-done((bf16[2,128,1536]{2,1,0:T(8,128)(2,1)S(1)}, bf16[2,128,1536]{2,1,0:T(8,128)(2,1)S(1)}, u32[]{:S(2)}, u32[]{:S(2)}) %collective-permute-start.21) | collective-permute-done | bytes 786464 | tf_op jit(solution)/shard_map/ppermute | solution.py:24
  343.0 10.0 %collective-permute-done.22.later_ref = bf16[2,128,1536]{2,1,0:T(8,128)(2,1)S(1)} collective-permute-done((bf16[2,128,1536]{2,1,0:T(8,128)(2,1)S(1)}, bf16[2,128,1536]{2,1,0:T(8,128)(2,1)S(1)}, u32[]{:S(2)}, u32[]{:S(2)}) %collective-permute-start.22) | collective-permute-done | bytes 786464 | tf_op jit(solution)/shard_map/ppermute | solution.py:24
  353.9 31.1 %leave.1 = (bf16[2,512,1920]{2,1,0:T(8,128)(2,1)}, f32[2,8,1792]{2,1,0:T(8,128)}, f32[2,8,1792]{2,1,0:T(8,128)}) custom-call(f32[2,512,1536]{2,1,0:T(8,128)} %get-tuple-element.77.y_ref, bf16[2,512,1536]{2,1,0:T(8,128)(2,1)} %get-tuple-element.55.x_ref, bf16[2,512,1536]{2,1,0:T(8,128)(2,1)} %get-tuple-element.76.g_ref, ...), custom_call_target="tpu_custom_call" | custom-call | flops 2000000000 | bytes 40000000 | tf_op jit(solution)/shard_map/leave/pallas_call | solution.py:717
  387.6 4.7 %fusion.2 = bf16[2,512,1536]{2,1,0:T(8,128)(2,1)} fusion(bf16[2,512,1536]{2,1,0:T(8,128)(2,1)S(1)} %copy-done, f32[1,512,1536]{2,1,0:T(8,128)} %add_bitcast_fusion.2, f32[1,512,1536]{2,1,0:T(8,128)} %add_bitcast_fusion.3, f32[2,512]{1,0:T(2,128)} %copy-done.36, bf16[2,512,16]{1,2,0:T(8,128)(2,1)S(1)} %copy-done.30, bf16[2,16,1536]{2,0,1:T(2,128)(2,1)S(1)} %copy-done.19), kind=kOutput, calls=%fused_computation.8 | convolution fusion | flops 59768832 | bytes 12718080 | tf_op jit(solution)/shard_map/str,srd->std/dot_general | solution.py:880
  399.0 5.9 %fusion.8 = f32[512,1536]{1,0:T(8,128)S(1)} fusion(bf16[1536,1920]{1,0:T(8,128)(2,1)} %get-tuple-element.90, bf16[2,512,1920]{2,1,0:T(8,128)(2,1)S(1)} %fusion.48), kind=kOutput, calls=%fused_computation.31 | convolution fusion | flops 3019898880 | bytes 11010048 | tf_op jit(solution)/shard_map/dot_general | solution.py:919
  408.5 7.7 %collective-permute-done.28 = bf16[2,32,1536]{2,1,0:T(8,128)(2,1)S(1)} collective-permute-done((bf16[2,32,1536]{2,1,0:T(8,128)(2,1)S(1)}, bf16[2,32,1536]{2,1,0:T(8,128)(2,1)S(1)}, u32[]{:S(2)}, u32[]{:S(2)}) %collective-permute-start.28) | collective-permute-done | bytes 196640 | tf_op jit(solution)/shard_map/ppermute | solution.py:33
  424.8 8.4 %collective-permute-done.30 = bf16[4,32,1536]{2,1,0:T(8,128)(2,1)S(1)} collective-permute-done((bf16[4,32,1536]{2,1,0:T(8,128)(2,1)S(1)}, bf16[4,32,1536]{2,1,0:T(8,128)(2,1)S(1)}, u32[]{:S(2)}, u32[]{:S(2)}) %collective-permute-start.30) | collective-permute-done | bytes 393248 | tf_op jit(solution)/shard_map/ppermute | solution.py:33
  (265 shorter events, 161.6 us)
Async XLA Ops:
  8.0 35.6 %collective-permute-start.2 = (bf16[384,1920]{1,0:T(8,128)(2,1)}, bf16[384,1920]{1,0:T(8,128)(2,1)}, u32[]{:S(2)}, u32[]{:S(2)}) collective-permute-start(bf16[384,1920]{1,0:T(8,128)(2,1)} %concatenate.38.w0), channel_id=1, source_target_pairs={{0,16},{8,24},{16,0},{24,8},{1,17},{9,25},{17,1},{25,9},{2,18},{10... | collective-permute-start | bytes 4423688 | tf_op jit(solution)/shard_map/ppermute | solution.py:33
  11.0 35.6 %collective-permute-start.1 = (bf16[384,1920]{1,0:T(8,128)(2,1)}, bf16[384,1920]{1,0:T(8,128)(2,1)}, u32[]{:S(2)}, u32[]{:S(2)}) collective-permute-start(bf16[384,1920]{1,0:T(8,128)(2,1)} %concatenate.38.w0), channel_id=1, source_target_pairs={{0,8},{8,0},{16,24},{24,16},{1,9},{9,1},{17,25},{25,17},{2,10},{10... | collective-permute-start | bytes 4423688 | tf_op jit(solution)/shard_map/ppermute | solution.py:33
  13.9 53.0 %collective-permute-start = (bf16[2,8,1536]{2,1,0:T(8,128)(2,1)}, bf16[2,8,1536]{2,1,0:T(8,128)(2,1)}, u32[]{:S(2)}, u32[]{:S(2)}) collective-permute-start(bf16[2,8,1536]{2,1,0:T(8,128)(2,1)} %slice.86), channel_id=1, source_target_pairs={{0,2},{2,4},{4,6},{1,3},{3,5},{5,7},{8,10},{10,12},{12,14},{9,11},... | collective-permute-start | bytes 147464 | tf_op jit(solution)/shard_map/ppermute | solution.py:24
  44.7 17.7 %collective-permute-start.4 = (bf16[192,1920]{1,0:T(8,128)(2,1)S(1)}, bf16[192,1920]{1,0:T(8,128)(2,1)S(1)}, u32[]{:S(2)}, u32[]{:S(2)}) collective-permute-start(bf16[192,1920]{1,0:T(8,128)(2,1)S(1)} %slice.115), channel_id=1, source_target_pairs={{0,8},{8,0},{16,24},{24,16},{1,9},{9,1},{17,25},{25,17},{2,10},{10... | collective-permute-start | bytes 2211848 | tf_op jit(solution)/shard_map/ppermute | solution.py:33
  47.7 17.2 %collective-permute-start.3 = (bf16[192,1920]{1,0:T(8,128)(2,1)S(1)}, bf16[192,1920]{1,0:T(8,128)(2,1)S(1)}, u32[]{:S(2)}, u32[]{:S(2)}) collective-permute-start(bf16[192,1920]{1,0:T(8,128)(2,1)S(1)} %slice.114), channel_id=1, source_target_pairs={{0,16},{8,24},{16,0},{24,8},{1,17},{9,25},{17,1},{25,9},{2,18},{10... | collective-permute-start | bytes 2211848 | tf_op jit(solution)/shard_map/ppermute | solution.py:33
  64.9 60.8 %collective-permute-start.9 = (bf16[384,1536]{1,0:T(8,128)(2,1)}, bf16[384,1536]{1,0:T(8,128)(2,1)}, u32[]{:S(2)}, u32[]{:S(2)}) collective-permute-start(bf16[384,1536]{1,0:T(8,128)(2,1)} %w0.1), channel_id=1, source_target_pairs={{0,16},{8,24},{16,0},{24,8},{1,17},{9,25},{17,1},{25,9},{2,18},{10... | collective-permute-start | bytes 3538952 | tf_op jit(solution)/shard_map/ppermute | solution.py:33
  66.4 59.3 %collective-permute-start.8 = (bf16[384,1536]{1,0:T(8,128)(2,1)}, bf16[384,1536]{1,0:T(8,128)(2,1)}, u32[]{:S(2)}, u32[]{:S(2)}) collective-permute-start(bf16[384,1536]{1,0:T(8,128)(2,1)} %w0.1), channel_id=1, source_target_pairs={{0,8},{8,0},{16,24},{24,16},{1,9},{9,1},{17,25},{25,17},{2,10},{10... | collective-permute-start | bytes 3538952 | tf_op jit(solution)/shard_map/ppermute | solution.py:33
  99.9 18.0 %collective-permute-start.5 = (bf16[2,128,1536]{2,1,0:T(8,128)(2,1)}, bf16[2,128,1536]{2,1,0:T(8,128)(2,1)}, u32[]{:S(2)}, u32[]{:S(2)}) collective-permute-start(bf16[2,128,1536]{2,1,0:T(8,128)(2,1)} %fusion.22), channel_id=1, source_target_pairs={{0,2},{2,4},{4,6},{1,3},{3,5},{5,7},{8,10},{10,12},{12,14},{9,11},... | collective-permute-start | bytes 2359304 | tf_op jit(solution)/shard_map/ppermute | solution.py:24
  120.1 40.6 %collective-permute-start.6 = (bf16[2,128,1536]{2,1,0:T(8,128)(2,1)}, bf16[2,128,1536]{2,1,0:T(8,128)(2,1)}, u32[]{:S(2)}, u32[]{:S(2)}) collective-permute-start(bf16[2,128,1536]{2,1,0:T(8,128)(2,1)} %add_convert_fusion.3), channel_id=1, source_target_pairs={{0,2},{2,4},{4,6},{1,3},{3,5},{5,7},{8,10},{10,12},{12,14},{9,11},... | collective-permute-start | bytes 2359304 | tf_op jit(solution)/shard_map/ppermute | solution.py:24
  125.7 29.2 %collective-permute-start.11 = (bf16[384,1536]{1,0:T(8,128)(2,1)}, bf16[384,1536]{1,0:T(8,128)(2,1)}, u32[]{:S(2)}, u32[]{:S(2)}) collective-permute-start(bf16[384,1536]{1,0:T(8,128)(2,1)} %w0), channel_id=1, source_target_pairs={{0,16},{8,24},{16,0},{24,8},{1,17},{9,25},{17,1},{25,9},{2,18},{10... | collective-permute-start | bytes 3538952 | tf_op jit(solution)/shard_map/ppermute | solution.py:33
  126.6 31.7 %collective-permute-start.10 = (bf16[384,1536]{1,0:T(8,128)(2,1)}, bf16[384,1536]{1,0:T(8,128)(2,1)}, u32[]{:S(2)}, u32[]{:S(2)}) collective-permute-start(bf16[384,1536]{1,0:T(8,128)(2,1)} %w0), channel_id=1, source_target_pairs={{0,8},{8,0},{16,24},{24,16},{1,9},{9,1},{17,25},{25,17},{2,10},{10... | collective-permute-start | bytes 3538952 | tf_op jit(solution)/shard_map/ppermute | solution.py:33
  141.4 26.9 %collective-permute-start.15 = (bf16[192,1536]{1,0:T(8,128)(2,1)S(1)}, bf16[192,1536]{1,0:T(8,128)(2,1)S(1)}, u32[]{:S(2)}, u32[]{:S(2)}) collective-permute-start(bf16[192,1536]{1,0:T(8,128)(2,1)S(1)} %slice.120), channel_id=1, source_target_pairs={{0,8},{8,0},{16,24},{24,16},{1,9},{9,1},{17,25},{25,17},{2,10},{10... | collective-permute-start | bytes 1769480 | tf_op jit(solution)/shard_map/ppermute | solution.py:33
  143.4 25.7 %collective-permute-start.14 = (bf16[192,1536]{1,0:T(8,128)(2,1)S(1)}, bf16[192,1536]{1,0:T(8,128)(2,1)}, u32[]{:S(2)}, u32[]{:S(2)}) collective-permute-start(bf16[192,1536]{1,0:T(8,128)(2,1)S(1)} %slice.119), channel_id=1, source_target_pairs={{0,16},{8,24},{16,0},{24,8},{1,17},{9,25},{17,1},{25,9},{2,18},{10... | collective-permute-start | bytes 1769480 | tf_op jit(solution)/shard_map/ppermute | solution.py:33
  156.8 26.3 %collective-permute-start.13 = (bf16[192,1536]{1,0:T(8,128)(2,1)}, bf16[192,1536]{1,0:T(8,128)(2,1)}, u32[]{:S(2)}, u32[]{:S(2)}) collective-permute-start(bf16[192,1536]{1,0:T(8,128)(2,1)} %slice.118), channel_id=1, source_target_pairs={{0,8},{8,0},{16,24},{24,16},{1,9},{9,1},{17,25},{25,17},{2,10},{10... | collective-permute-start | bytes 1769480 | tf_op jit(solution)/shard_map/ppermute | solution.py:33
  160.2 22.9 %collective-permute-start.12 = (bf16[192,1536]{1,0:T(8,128)(2,1)}, bf16[192,1536]{1,0:T(8,128)(2,1)}, u32[]{:S(2)}, u32[]{:S(2)}) collective-permute-start(bf16[192,1536]{1,0:T(8,128)(2,1)} %slice.117), channel_id=1, source_target_pairs={{0,16},{8,24},{16,0},{24,8},{1,17},{9,25},{17,1},{25,9},{2,18},{10... | collective-permute-start | bytes 1769480 | tf_op jit(solution)/shard_map/ppermute | solution.py:33
  162.9 35.1 %collective-permute-start.7 = (bf16[2,128,1536]{2,1,0:T(8,128)(2,1)}, bf16[2,128,1536]{2,1,0:T(8,128)(2,1)S(1)}, u32[]{:S(2)}, u32[]{:S(2)}) collective-permute-start(bf16[2,128,1536]{2,1,0:T(8,128)(2,1)} %add_convert_fusion.2), channel_id=1, source_target_pairs={{0,2},{2,4},{4,6},{1,3},{3,5},{5,7},{8,10},{10,12},{12,14},{9,11},... | collective-permute-start | bytes 2359304 | tf_op jit(solution)/shard_map/ppermute | solution.py:24
  252.6 59.2 %collective-permute-start.20 = (bf16[2,128,1536]{2,1,0:T(8,128)(2,1)S(1)}, bf16[2,128,1536]{2,1,0:T(8,128)(2,1)}, u32[]{:S(2)}, u32[]{:S(2)}) collective-permute-start(bf16[2,128,1536]{2,1,0:T(8,128)(2,1)S(1)} %copy-done.12), channel_id=1, source_target_pairs={{2,0},{4,2},{6,4},{3,1},{5,3},{7,5},{10,8},{12,10},{14,12},{11,9},... | collective-permute-start | bytes 2359304 | tf_op jit(solution)/shard_map/ppermute | solution.py:24
  254.1 80.9 %collective-permute-start.17 = (bf16[512,1536]{1,0:T(8,128)(2,1)}, bf16[512,1536]{1,0:T(8,128)(2,1)}, u32[]{:S(2)}, u32[]{:S(2)}) collective-permute-start(bf16[512,1536]{1,0:T(8,128)(2,1)} %convolution_convert_fusion.1), channel_id=1, source_target_pairs={{0,1},{1,0},{2,3},{3,2},{4,5},{5,4},{6,7},{7,6},{8,9},{9,8},{10,11... | collective-permute-start | bytes 4718600 | tf_op jit(solution)/shard_map/ppermute | solution.py:29
  254.3 84.6 %collective-permute-start.18 = (bf16[512,1536]{1,0:T(8,128)(2,1)}, bf16[512,1536]{1,0:T(8,128)(2,1)}, u32[]{:S(2)}, u32[]{:S(2)}) collective-permute-start(bf16[512,1536]{1,0:T(8,128)(2,1)} %convolution_convert_fusion), channel_id=1, source_target_pairs={{0,1},{1,0},{2,3},{3,2},{4,5},{5,4},{6,7},{7,6},{8,9},{9,8},{10,11... | collective-permute-start | bytes 4718600 | tf_op jit(solution)/shard_map/ppermute | solution.py:29
  257.2 26.5 %collective-permute-start.31 = (bf16[2,48,1536]{2,1,0:T(8,128)(2,1)}, bf16[2,48,1536]{2,1,0:T(8,128)(2,1)}, u32[]{:S(2)}, u32[]{:S(2)}) collective-permute-start(bf16[2,48,1536]{2,1,0:T(8,128)(2,1)} %pad_maximum_fusion.5), channel_id=1, source_target_pairs={{0,2},{2,0},{4,6},{6,4},{1,3},{3,1},{5,7},{7,5},{8,10},{10,8},{12,... | collective-permute-start | bytes 884744 | tf_op jit(solution)/shard_map/ppermute | solution.py:33
  284.7 15.7 %collective-permute-start.32 = (bf16[2,48,1536]{2,1,0:T(8,128)(2,1)S(1)}, bf16[2,48,1536]{2,1,0:T(8,128)(2,1)S(1)}, u32[]{:S(2)}, u32[]{:S(2)}) collective-permute-start(bf16[2,48,1536]{2,1,0:T(8,128)(2,1)S(1)} %add_convert_fusion.5), channel_id=1, source_target_pairs={{0,4},{2,6},{4,0},{6,2},{1,5},{3,7},{5,1},{7,3},{8,12},{10,14},{12... | collective-permute-start | bytes 884744 | tf_op jit(solution)/shard_map/ppermute | solution.py:33
  313.2 20.2 %collective-permute-start.21 = (bf16[2,128,1536]{2,1,0:T(8,128)(2,1)S(1)}, bf16[2,128,1536]{2,1,0:T(8,128)(2,1)S(1)}, u32[]{:S(2)}, u32[]{:S(2)}) collective-permute-start(bf16[2,128,1536]{2,1,0:T(8,128)(2,1)S(1)} %fusion.10), channel_id=1, source_target_pairs={{2,0},{4,2},{6,4},{3,1},{5,3},{7,5},{10,8},{12,10},{14,12},{11,9},... | collective-permute-start | bytes 2359304 | tf_op jit(solution)/shard_map/ppermute | solution.py:24
  333.7 19.4 %collective-permute-start.22 = (bf16[2,128,1536]{2,1,0:T(8,128)(2,1)S(1)}, bf16[2,128,1536]{2,1,0:T(8,128)(2,1)S(1)}, u32[]{:S(2)}, u32[]{:S(2)}) collective-permute-start(bf16[2,128,1536]{2,1,0:T(8,128)(2,1)S(1)} %fusion.11), channel_id=1, source_target_pairs={{2,0},{4,2},{6,4},{3,1},{5,3},{7,5},{10,8},{12,10},{14,12},{11,9},... | collective-permute-start | bytes 2359304 | tf_op jit(solution)/shard_map/ppermute | solution.py:24
  418.6 18.8 %collective-permute-start.25 = (bf16[512,1536]{1,0:T(8,128)(2,1)S(1)}, bf16[512,1536]{1,0:T(8,128)(2,1)S(1)}, u32[]{:S(2)}, u32[]{:S(2)}) collective-permute-start(bf16[512,1536]{1,0:T(8,128)(2,1)S(1)} %add_convert_fusion), channel_id=1, source_target_pairs={{0,1},{1,0},{2,3},{3,2},{4,5},{5,4},{6,7},{7,6},{8,9},{9,8},{10,11... | collective-permute-start | bytes 4718600 | tf_op jit(solution)/shard_map/ppermute | solution.py:29
  (65 other events, 730.4 us)
